TPU v7x, 256 devices: a whole 4x4x8 slice. The times are simulated.
256 devices in a mesh: frame: 32 (over z_hi, y, x), head: 8 (over z_lo, core).
Axes of the slice: x: 4, y: 4, z: 8 (z_hi: 2, z_lo: 4; z = z_hi * 4 + z_lo), core: 2. Of those that a mesh axis runs over, the one named last changes fastest.
Arguments:
- queries: bfloat16 [8192, 5120], P('frame', 'head'), may hold values from -12 to 12
- keys: bfloat16 [8192, 5120], P('frame', 'head'), may hold values from -12 to 12
- values: bfloat16 [8192, 5120], P('frame', 'head'), may hold values from -6 to 6
- policy_grad: bfloat16 [8192, 5120], P('frame', 'head'), may hold values from -6 to 6
- ref_velocity: bfloat16 [8192, 5120], P('frame', 'head'), may hold values from -6 to 6
- key_lists: int32 [64, 6], P('frame'), may hold values from 0 to 63, as said below
- frame_tokens: int32 [64], replicated, may hold values from 32 to 128, as said below
Outputs:
- grad_queries: bfloat16 [8192, 5120], P('frame', 'head')
- grad_keys: bfloat16 [8192, 5120], P('frame', 'head')
- grad_values: bfloat16 [8192, 5120], P('frame', 'head')
Inputs may be any that keep to these rules, and one draw needn't show every extreme that they name: `key_lists`: row b holds 6 distinct blocks: b, the next block of the same index of frame (cyclic over its 2 blocks), and four blocks on indices of frame that differ from b's index by distinct signed powers of two. `frame_tokens`: some block is full.
All inputs are finite; a program needn't handle non-finite values.
Results may differ from a plain program's by a relative error of at most 0.011.
Values may be sent and summed in bfloat16 or wider, within the bound.
No kernel may reach another device: no remote copies, remote signals or barrier semaphores. Data moves between devices by JAX's collectives and lax.ppermute only.
A program may use at most 128 MiB of HBM per device.

v0:
```python
import math
import jax
import jax.numpy as jnp
from jax import lax
from jax.sharding import PartitionSpec as P

HEADS = 40
HD = 128
BLK = 128
kl_weight = 1.0


def from_behind(value, axis, steps):
    count = lax.axis_size(axis)
    leading, last = (max(0, -steps), min(count, count - steps))
    return lax.ppermute(value, axis, [(source, source + steps) for source in range(leading, last)])


def local(queries, keys, values, policy_grad, ref_velocity, key_lists, frame_tokens):
    rows, cols = queries.shape
    heads_here = cols // HD
    blocks_here = rows // BLK
    list_len = key_lists.shape[1]
    all_blocks = frame_tokens.shape[0]
    scale = 1.0 / math.sqrt(HD)
    levels = lax.axis_size("frame").bit_length() - 1
    me_index = lax.axis_index("frame")
    offsets = [0]
    pool_k = [keys]
    pool_v = [values]
    for level in range(levels):
        for sign in (1, -1):
            moved = from_behind((keys, values), "frame", sign * (1 << level))
            offsets.append(-sign * (1 << level))
            pool_k.append(moved[0])
            pool_v.append(moved[1])
    classes = len(offsets)
    pool_keys = jnp.stack(pool_k).reshape(classes * blocks_here, BLK, cols)
    pool_values = jnp.stack(pool_v).reshape(classes * blocks_here, BLK, cols)
    owner_gap = key_lists // blocks_here - me_index
    class_of = jnp.zeros_like(key_lists)
    for position, offset in enumerate(offsets):
        class_of = class_of + jnp.where(owner_gap == offset, position, 0)
    pool_index = class_of * blocks_here + key_lists % blocks_here
    key_block = pool_keys[pool_index].reshape(blocks_here, list_len * BLK, heads_here, HD)
    value_block = pool_values[pool_index].reshape(blocks_here, list_len * BLK, heads_here, HD)
    counts = jnp.sum(
        jnp.where(key_lists[..., None] == jnp.arange(all_blocks, dtype=jnp.int32), frame_tokens, 0),
        axis=-1,
    )
    valid = (jnp.arange(BLK, dtype=jnp.int32)[None, None, :] < counts[..., None]).reshape(
        blocks_here, list_len * BLK
    )
    query4 = queries.reshape(blocks_here, BLK, heads_here, HD)
    scores = (
        jnp.einsum("bqhd,bkhd->bhqk", query4, key_block, preferred_element_type=jnp.float32) * scale
    )
    scores = jnp.where(valid[:, None, None, :], scores, -1e30)
    highest = jnp.max(scores, axis=-1, keepdims=True)
    expd = jnp.exp(scores - highest)
    probs = expd / jnp.sum(expd, axis=-1, keepdims=True)
    probs16 = probs.astype(jnp.bfloat16)
    attn = jnp.einsum("bhqk,bkhd->bqhd", probs16, value_block, preferred_element_type=jnp.float32)
    diff = attn - ref_velocity.reshape(blocks_here, BLK, heads_here, HD).astype(jnp.float32)
    squares = lax.psum(jnp.sum(diff * diff, axis=(2, 3)), "head")
    kl = squares / (HEADS * HD)
    upstream = (
        policy_grad.reshape(blocks_here, BLK, heads_here, HD).astype(jnp.float32)
        + kl_weight * diff / (1.0 + kl)[:, :, None, None]
    )
    grad16 = upstream.astype(jnp.bfloat16)
    grad_probs = jnp.einsum(
        "bqhd,bkhd->bhqk", grad16, value_block, preferred_element_type=jnp.float32
    )
    delta = jnp.transpose(jnp.sum(grad16.astype(jnp.float32) * attn, axis=-1), (0, 2, 1))
    grad_scores16 = (probs * (grad_probs - delta[..., None])).astype(jnp.bfloat16)
    grad_q = (
        jnp.einsum("bhqk,bkhd->bqhd", grad_scores16, key_block, preferred_element_type=jnp.float32)
        * scale
    ).astype(jnp.bfloat16)
    part_k = (
        jnp.einsum("bhqk,bqhd->bkhd", grad_scores16, query4, preferred_element_type=jnp.float32)
        * scale
    )
    part_v = jnp.einsum("bhqk,bqhd->bkhd", probs16, grad16, preferred_element_type=jnp.float32)
    part_k = part_k.reshape(blocks_here * list_len, BLK * cols)
    part_v = part_v.reshape(blocks_here * list_len, BLK * cols)
    flat_index = pool_index.reshape(-1)
    selector = (
        jnp.arange(classes * blocks_here, dtype=jnp.int32)[:, None] == flat_index[None, :]
    ).astype(jnp.float32)
    pooled_k = jnp.dot(selector, part_k, precision=lax.Precision.HIGHEST).reshape(
        classes, blocks_here, BLK * cols
    )
    pooled_v = jnp.dot(selector, part_v, precision=lax.Precision.HIGHEST).reshape(
        classes, blocks_here, BLK * cols
    )
    total_k = pooled_k[0]
    total_v = pooled_v[0]
    for position in range(1, classes):
        back = from_behind(
            (pooled_k[position].astype(jnp.bfloat16), pooled_v[position].astype(jnp.bfloat16)),
            "frame",
            offsets[position],
        )
        total_k = total_k + back[0].astype(jnp.float32)
        total_v = total_v + back[1].astype(jnp.float32)
    grad_queries = grad_q.reshape(rows, cols)
    grad_keys = total_k.reshape(rows, cols).astype(jnp.bfloat16)
    grad_values = total_v.reshape(rows, cols).astype(jnp.bfloat16)
    return (grad_queries, grad_keys, grad_values)


def solution(mesh):
    in_specs = (
        P("frame", "head"),
        P("frame", "head"),
        P("frame", "head"),
        P("frame", "head"),
        P("frame", "head"),
        P("frame", None),
        P(),
    )
    out_specs = (P("frame", "head"), P("frame", "head"), P("frame", "head"))
    return jax.shard_map(local, mesh=mesh, in_specs=in_specs, out_specs=out_specs, check_vma=False)
```

profile of v0, /device:TPU:94, one launch (start us, length us, event | category | flops | bytes accessed | tf_op | source)
XLA Modules:
  0.0 415.7 jit_solution(6033962399658650368)
XLA Ops:
  0.7 7.0 %collective-permute-start = (bf16[256,640]{1,0:T(8,128)(2,1)}, bf16[256,640]{1,0:T(8,128)(2,1)}, u32[]{:S(2)}, u32[]{:S(2)}) collective-permute-start(bf16[256,640]{1,0:T(8,128)(2,1)} %param.8), channel_id=1, source_target_pairs={{0,8},{8,16},{16,24},{24,32},{32,40},{40,48},{48,56},{56,64},{64,7... | collective-permute-start | bytes 983048 | tf_op jit(solution)/shard_map/ppermute | solution.py:16
  7.7 1.9 collective-permute-start.1
  9.6 4.9 %collective-permute-start.2 = (bf16[256,640]{1,0:T(8,128)(2,1)}, bf16[256,640]{1,0:T(8,128)(2,1)}, u32[]{:S(2)}, u32[]{:S(2)}) collective-permute-start(bf16[256,640]{1,0:T(8,128)(2,1)} %param.8), channel_id=1, source_target_pairs={{0,16},{8,24},{16,32},{24,40},{32,48},{40,56},{48,64},{56,72},{64,... | collective-permute-start | bytes 983048 | tf_op jit(solution)/shard_map/ppermute | solution.py:16
  14.5 2.5 collective-permute-start.3
  17.0 4.0 collective-permute-start.4
  29.1 8.1 %collective-permute-done = bf16[256,640]{1,0:T(8,128)(2,1)} collective-permute-done((bf16[256,640]{1,0:T(8,128)(2,1)}, bf16[256,640]{1,0:T(8,128)(2,1)}, u32[]{:S(2)}, u32[]{:S(2)}) %collective-permute-start) | collective-permute-done | bytes 327712 | tf_op jit(solution)/shard_map/ppermute | solution.py:16
  37.1 1.9 collective-permute-start.5
  40.8 2.2 collective-permute-done.1
  43.0 1.9 collective-permute-start.6
  46.7 11.4 %collective-permute-done.2 = bf16[256,640]{1,0:T(8,128)(2,1)} collective-permute-done((bf16[256,640]{1,0:T(8,128)(2,1)}, bf16[256,640]{1,0:T(8,128)(2,1)}, u32[]{:S(2)}, u32[]{:S(2)}) %collective-permute-start.2) | collective-permute-done | bytes 327712 | tf_op jit(solution)/shard_map/ppermute | solution.py:16
  58.1 1.9 collective-permute-start.7
  64.8 2.8 collective-permute-done.4
  70.6 15.9 %collective-permute-start.10 = (bf16[256,640]{1,0:T(8,128)(2,1)S(1)}, bf16[256,640]{1,0:T(8,128)(2,1)S(1)}, u32[]{:S(2)}, u32[]{:S(2)}) collective-permute-start(bf16[256,640]{1,0:T(8,128)(2,1)S(1)} %copy-done.18), channel_id=1, source_target_pairs={{0,8},{8,16},{16,24},{24,32},{32,40},{40,48},{48,56},{56,64},{64,7... | collective-permute-start | bytes 983048 | tf_op jit(solution)/shard_map/ppermute | solution.py:16
  87.3 1.9 collective-permute-start.11
  90.0 7.6 %collective-permute-start.12 = (bf16[256,640]{1,0:T(8,128)(2,1)S(1)}, bf16[256,640]{1,0:T(8,128)(2,1)S(1)}, u32[]{:S(2)}, u32[]{:S(2)}) collective-permute-start(bf16[256,640]{1,0:T(8,128)(2,1)S(1)} %copy-done.18), channel_id=1, source_target_pairs={{0,16},{8,24},{16,32},{24,40},{32,48},{40,56},{48,64},{56,72},{64,... | collective-permute-start | bytes 983048 | tf_op jit(solution)/shard_map/ppermute | solution.py:16
  98.4 1.9 collective-permute-start.13
  101.0 2.5 collective-permute-start.14
  104.3 24.1 %collective-permute-done.10 = bf16[256,640]{1,0:T(8,128)(2,1)S(1)} collective-permute-done((bf16[256,640]{1,0:T(8,128)(2,1)S(1)}, bf16[256,640]{1,0:T(8,128)(2,1)S(1)}, u32[]{:S(2)}, u32[]{:S(2)}) %collective-permute-start.10) | collective-permute-done | bytes 327712 | tf_op jit(solution)/shard_map/ppermute | solution.py:16
  131.0 1.9 collective-permute-start.16
  133.7 2.3 collective-permute-done.12
  136.0 3.1 collective-permute-start.17
  139.9 2.0 collective-permute-start.18
  142.7 4.5 %collective-permute-done.14 = bf16[256,640]{1,0:T(8,128)(2,1)S(1)} collective-permute-done((bf16[256,640]{1,0:T(8,128)(2,1)S(1)}, bf16[256,640]{1,0:T(8,128)(2,1)S(1)}, u32[]{:S(2)}, u32[]{:S(2)}) %collective-permute-start.14) | collective-permute-done | bytes 327712 | tf_op jit(solution)/shard_map/ppermute | solution.py:16
  149.2 3.0 collective-permute-done.15
  153.0 3.8 collective-permute-done.16
  158.3 2.9 gather_fusion
  161.3 3.5 reshape.143
  164.8 3.5 copy.77
  171.7 4.3 %gather_fusion.1 = bf16[12,128,640]{2,1,0:T(8,128)(2,1)} fusion(bf16[22,128,640]{2,1,0:T(8,128)(2,1)} %bitcast.86, s32[1024]{0:T(1024)S(1)} %pad_clamp_fusion), kind=kCustom, calls=%fused_computation.1 | custom fusion | bytes 3932208 | tf_op jit(solution)/shard_map/gather | solution.py:46
  175.9 5.6 %reshape.144 = bf16[2,768,5,128]{3,2,1,0:T(8,128)(2,1)} reshape(bf16[12,128,640]{2,1,0:T(8,128)(2,1)} %gather_fusion.1) | data formatting | bytes 3932160 | tf_op jit(solution)/shard_map/reshape | solution.py:46
  184.3 2.1 multiply_reduce_fusion.1
  186.5 10.3 %psum.7 = f32[2,128]{1,0:T(2,128)S(1)} all-reduce(f32[2,128]{1,0:T(2,128)S(1)} %get-tuple-element.14), channel_id=1, replica_groups=mesh['frame'=32,'head'=8] {'head'}, use_global_device_ids=true, to_apply=%region_4.5 | all-reduce | flops 256 | bytes 2048 | tf_op jit(solution)/shard_map/psum | solution.py:65
  198.2 4.9 %convolution_bitcast_fusion = f32[2,768,5,128]{1,3,2,0:T(8,128)} fusion(bf16[2,128,5,128]{1,3,2,0:T(8,128)(2,1)S(1)} %get-tuple-element.13, f32[2,5,128,768]{2,3,1,0:T(8,128)} %copy-done.21, f32[2,5,128]{2,1,0:T(8,128)S(1)} %get-tuple-element.38), kind=kOutput, calls=%fused_computation.10 | convolution fusion | flops 253624320 | bytes 8197120 | tf_op jit(solution)/shard_map/bhqk,bqhd->bkhd/dot_general | solution.py:85
  206.0 5.0 %copy.81 = f32[2,768,5,128]{3,2,1,0:T(8,128)} copy(f32[2,768,5,128]{3,1,2,0:T(8,128)S(1)} %multiply_bitcast_fusion) | data formatting | bytes 7864320 | tf_op jit(solution)/shard_map/mul | solution.py:82
  211.0 5.4 %reshape.113 = f32[12,81920]{1,0:T(8,128)} reshape(f32[2,768,5,128]{3,2,1,0:T(8,128)} %copy.81) | data formatting | bytes 7864320 | tf_op jit(solution)/shard_map/reshape | solution.py:86
  216.4 9.0 %fusion.48 = (bf16[22,81920]{1,0:T(8,128)(2,1)S(1)}, f32[22,81920]{1,0:T(8,128)}) fusion(f32[12,81920]{1,0:T(8,128)} %reshape.113, s32[12]{0:T(128)S(1)} %eq.75), kind=kOutput, calls=%fused_computation.109 | convolution fusion | flops 261325056 | bytes 14745648 | tf_op jit(solution)/shard_map/dot_general | solution.py:92
  225.4 3.8 fusion.46
  229.2 3.2 collective-permute-start.29
  233.7 16.1 %collective-permute-start.27 = (bf16[2,81920]{1,0:T(2,128)(2,1)}, bf16[2,81920]{1,0:T(2,128)(2,1)S(1)}, u32[]{:S(2)}, u32[]{:S(2)}) collective-permute-start(bf16[2,81920]{1,0:T(2,128)(2,1)} %get-tuple-element.31), channel_id=1, source_target_pairs={{0,64},{8,72},{16,80},{24,88},{32,96},{40,104},{48,112},{56,120},{... | collective-permute-start | bytes 983048 | tf_op jit(solution)/shard_map/ppermute | solution.py:16
  249.8 1.9 collective-permute-start.26
  251.8 10.8 %collective-permute-start.25 = (bf16[2,81920]{1,0:T(2,128)(2,1)}, bf16[2,81920]{1,0:T(2,128)(2,1)}, u32[]{:S(2)}, u32[]{:S(2)}) collective-permute-start(bf16[2,81920]{1,0:T(2,128)(2,1)} %get-tuple-element.33), channel_id=1, source_target_pairs={{0,32},{8,40},{16,48},{24,56},{32,64},{40,72},{48,80},{56,88},{64,... | collective-permute-start | bytes 983048 | tf_op jit(solution)/shard_map/ppermute | solution.py:16
  262.5 6.0 %copy.83 = f32[2,768,5,128]{3,2,1,0:T(8,128)} copy(f32[2,768,5,128]{1,3,2,0:T(8,128)} %convolution_bitcast_fusion) | data formatting | bytes 7864320 | tf_op jit(solution)/shard_map/bhqk,bqhd->bkhd/transpose | solution.py:85
  268.5 5.3 %reshape.114 = f32[12,81920]{1,0:T(8,128)} reshape(f32[2,768,5,128]{3,2,1,0:T(8,128)} %copy.83) | data formatting | bytes 7864320 | tf_op jit(solution)/shard_map/reshape | solution.py:87
  273.9 9.1 %fusion.49 = (bf16[22,81920]{1,0:T(8,128)(2,1)S(1)}, f32[22,81920]{1,0:T(8,128)}) fusion(f32[12,81920]{1,0:T(8,128)} %reshape.114, s32[12]{0:T(128)S(1)} %eq.75), kind=kOutput, calls=%fused_computation.110 | convolution fusion | flops 261325056 | bytes 14745648 | tf_op jit(solution)/shard_map/dot_general | solution.py:95
  283.0 2.1 collective-permute-start.24
  285.1 13.1 %collective-permute-start.23 = (bf16[2,81920]{1,0:T(2,128)(2,1)S(1)}, bf16[2,81920]{1,0:T(2,128)(2,1)S(1)}, u32[]{:S(2)}, u32[]{:S(2)}) collective-permute-start(bf16[2,81920]{1,0:T(2,128)(2,1)S(1)} %copy-done.14), channel_id=1, source_target_pairs={{0,16},{8,24},{16,32},{24,40},{32,48},{40,56},{48,64},{56,72},{64,... | collective-permute-start | bytes 983048 | tf_op jit(solution)/shard_map/ppermute | solution.py:16
  298.1 1.9 collective-permute-start.22
  300.1 13.3 %collective-permute-start.21 = (bf16[2,81920]{1,0:T(2,128)(2,1)S(1)}, bf16[2,81920]{1,0:T(2,128)(2,1)S(1)}, u32[]{:S(2)}, u32[]{:S(2)}) collective-permute-start(bf16[2,81920]{1,0:T(2,128)(2,1)S(1)} %copy-done.12), channel_id=1, source_target_pairs={{0,8},{8,16},{16,24},{24,32},{32,40},{40,48},{48,56},{56,64},{64,7... | collective-permute-start | bytes 983048 | tf_op jit(solution)/shard_map/ppermute | solution.py:16
  313.4 1.9 collective-permute-start.20
  315.3 3.8 fusion.45
  319.2 2.0 collective-permute-start.39
  323.4 1.9 collective-permute-start.37
  325.3 14.8 %collective-permute-done.21 = bf16[2,81920]{1,0:T(2,128)(2,1)S(1)} collective-permute-done((bf16[2,81920]{1,0:T(2,128)(2,1)S(1)}, bf16[2,81920]{1,0:T(2,128)(2,1)S(1)}, u32[]{:S(2)}, u32[]{:S(2)}) %collective-permute-start.21) | collective-permute-done | bytes 327712 | tf_op jit(solution)/shard_map/ppermute | solution.py:16
  340.1 1.9 collective-permute-start.36
  342.0 1.9 collective-permute-start.35
  345.8 9.1 %collective-permute-done.39 = bf16[2,81920]{1,0:T(2,128)(2,1)} collective-permute-done((bf16[2,81920]{1,0:T(2,128)(2,1)}, bf16[2,81920]{1,0:T(2,128)(2,1)}, u32[]{:S(2)}, u32[]{:S(2)}) %collective-permute-start.39) | collective-permute-done | bytes 327712 | tf_op jit(solution)/shard_map/ppermute | solution.py:16
  356.8 2.9 collective-permute-start.33
  359.7 9.2 %collective-permute-done.37 = bf16[2,81920]{1,0:T(2,128)(2,1)} collective-permute-done((bf16[2,81920]{1,0:T(2,128)(2,1)}, bf16[2,81920]{1,0:T(2,128)(2,1)}, u32[]{:S(2)}, u32[]{:S(2)}) %collective-permute-start.37) | collective-permute-done | bytes 327712 | tf_op jit(solution)/shard_map/ppermute | solution.py:16
  370.8 11.9 %collective-permute-start.31 = (bf16[2,81920]{1,0:T(2,128)(2,1)}, bf16[2,81920]{1,0:T(2,128)(2,1)S(1)}, u32[]{:S(2)}, u32[]{:S(2)}) collective-permute-start(bf16[2,81920]{1,0:T(2,128)(2,1)} %get-tuple-element.27), channel_id=1, source_target_pairs={{0,8},{8,16},{16,24},{24,32},{32,40},{40,48},{48,56},{56,64},{64,7... | collective-permute-start | bytes 983048 | tf_op jit(solution)/shard_map/ppermute | solution.py:16
  382.8 2.2 collective-permute-start.30
  384.9 4.1 add_convert_fusion.1
  390.0 5.5 %collective-permute-done.31 = bf16[2,81920]{1,0:T(2,128)(2,1)S(1)} collective-permute-done((bf16[2,81920]{1,0:T(2,128)(2,1)}, bf16[2,81920]{1,0:T(2,128)(2,1)S(1)}, u32[]{:S(2)}, u32[]{:S(2)}) %collective-permute-start.31) | collective-permute-done | bytes 327712 | tf_op jit(solution)/shard_map/ppermute | solution.py:16
  395.5 15.2 %collective-permute-done.30 = bf16[2,81920]{1,0:T(2,128)(2,1)S(1)} collective-permute-done((bf16[2,81920]{1,0:T(2,128)(2,1)}, bf16[2,81920]{1,0:T(2,128)(2,1)S(1)}, u32[]{:S(2)}, u32[]{:S(2)}) %collective-permute-start.30) | collective-permute-done | bytes 327712 | tf_op jit(solution)/shard_map/ppermute | solution.py:16
  410.7 4.0 add_convert_fusion
  (128 shorter events, 53.8 us)
Async XLA Ops:
  0.6 26.1 %copy-start.18 = (bf16[256,640]{1,0:T(8,128)(2,1)S(1)}, bf16[256,640]{1,0:T(8,128)(2,1)}, u32[]{:S(2)}) copy-start(bf16[256,640]{1,0:T(8,128)(2,1)} %param.9) | copy-start | bytes 983044
  0.6 26.9 %copy-start.16 = (bf16[256,640]{1,0:T(8,128)(2,1)S(1)}, bf16[256,640]{1,0:T(8,128)(2,1)}, u32[]{:S(2)}) copy-start(bf16[256,640]{1,0:T(8,128)(2,1)} %param.7) | copy-start | bytes 983044
  0.7 27.3 %copy-start.20 = (s32[64]{0:T(128)S(1)}, s32[64]{0:T(128)}, u32[]{:S(2)}) copy-start(s32[64]{0:T(128)} %param.13) | copy-start | bytes 772
  0.7 27.7 %copy-start.19 = (bf16[256,640]{1,0:T(8,128)(2,1)S(1)}, bf16[256,640]{1,0:T(8,128)(2,1)}, u32[]{:S(2)}) copy-start(bf16[256,640]{1,0:T(8,128)(2,1)} %param.10) | copy-start | bytes 983044
  0.7 36.5 %collective-permute-start = (bf16[256,640]{1,0:T(8,128)(2,1)}, bf16[256,640]{1,0:T(8,128)(2,1)}, u32[]{:S(2)}, u32[]{:S(2)}) collective-permute-start(bf16[256,640]{1,0:T(8,128)(2,1)} %param.8), channel_id=1, source_target_pairs={{0,8},{8,16},{16,24},{24,32},{32,40},{40,48},{48,56},{56,64},{64,7... | collective-permute-start | bytes 983048 | tf_op jit(solution)/shard_map/ppermute | solution.py:16
  7.7 35.3 %collective-permute-start.1 = (bf16[256,640]{1,0:T(8,128)(2,1)}, bf16[256,640]{1,0:T(8,128)(2,1)}, u32[]{:S(2)}, u32[]{:S(2)}) collective-permute-start(bf16[256,640]{1,0:T(8,128)(2,1)} %param.8), channel_id=1, source_target_pairs={{8,0},{16,8},{24,16},{32,24},{40,32},{48,40},{56,48},{64,56},{72,6... | collective-permute-start | bytes 983048 | tf_op jit(solution)/shard_map/ppermute | solution.py:16
  9.6 48.4 %collective-permute-start.2 = (bf16[256,640]{1,0:T(8,128)(2,1)}, bf16[256,640]{1,0:T(8,128)(2,1)}, u32[]{:S(2)}, u32[]{:S(2)}) collective-permute-start(bf16[256,640]{1,0:T(8,128)(2,1)} %param.8), channel_id=1, source_target_pairs={{0,16},{8,24},{16,32},{24,40},{32,48},{40,56},{48,64},{56,72},{64,... | collective-permute-start | bytes 983048 | tf_op jit(solution)/shard_map/ppermute | solution.py:16
  14.5 47.3 %collective-permute-start.3 = (bf16[256,640]{1,0:T(8,128)(2,1)}, bf16[256,640]{1,0:T(8,128)(2,1)}, u32[]{:S(2)}, u32[]{:S(2)}) collective-permute-start(bf16[256,640]{1,0:T(8,128)(2,1)} %param.8), channel_id=1, source_target_pairs={{16,0},{24,8},{32,16},{40,24},{48,32},{56,40},{64,48},{72,56},{80,... | collective-permute-start | bytes 983048 | tf_op jit(solution)/shard_map/ppermute | solution.py:16
  17.0 50.6 %collective-permute-start.4 = (bf16[256,640]{1,0:T(8,128)(2,1)}, bf16[256,640]{1,0:T(8,128)(2,1)}, u32[]{:S(2)}, u32[]{:S(2)}) collective-permute-start(bf16[256,640]{1,0:T(8,128)(2,1)} %param.8), channel_id=1, source_target_pairs={{0,32},{8,40},{16,48},{24,56},{32,64},{40,72},{48,80},{56,88},{64,... | collective-permute-start | bytes 983048 | tf_op jit(solution)/shard_map/ppermute | solution.py:16
  24.3 12.8 %copy-start.17 = (bf16[256,640]{1,0:T(8,128)(2,1)S(1)}, bf16[256,640]{1,0:T(8,128)(2,1)}, u32[]{:S(2)}) copy-start(bf16[256,640]{1,0:T(8,128)(2,1)} %param.8) | copy-start | bytes 983044
  37.1 33.4 %collective-permute-start.5 = (bf16[256,640]{1,0:T(8,128)(2,1)S(1)}, bf16[256,640]{1,0:T(8,128)(2,1)S(1)}, u32[]{:S(2)}, u32[]{:S(2)}) collective-permute-start(bf16[256,640]{1,0:T(8,128)(2,1)S(1)} %copy-done.17), channel_id=1, source_target_pairs={{32,0},{40,8},{48,16},{56,24},{64,32},{72,40},{80,48},{88,56},{96,... | collective-permute-start | bytes 983048 | tf_op jit(solution)/shard_map/ppermute | solution.py:16
  43.0 44.3 %collective-permute-start.6 = (bf16[256,640]{1,0:T(8,128)(2,1)S(1)}, bf16[256,640]{1,0:T(8,128)(2,1)S(1)}, u32[]{:S(2)}, u32[]{:S(2)}) collective-permute-start(bf16[256,640]{1,0:T(8,128)(2,1)S(1)} %copy-done.17), channel_id=1, source_target_pairs={{0,64},{8,72},{16,80},{24,88},{32,96},{40,104},{48,112},{56,120},{... | collective-permute-start | bytes 983048 | tf_op jit(solution)/shard_map/ppermute | solution.py:16
  58.1 31.9 %collective-permute-start.7 = (bf16[256,640]{1,0:T(8,128)(2,1)S(1)}, bf16[256,640]{1,0:T(8,128)(2,1)S(1)}, u32[]{:S(2)}, u32[]{:S(2)}) collective-permute-start(bf16[256,640]{1,0:T(8,128)(2,1)S(1)} %copy-done.17), channel_id=1, source_target_pairs={{64,0},{72,8},{80,16},{88,24},{96,32},{104,40},{112,48},{120,56},{... | collective-permute-start | bytes 983048 | tf_op jit(solution)/shard_map/ppermute | solution.py:16
  61.7 36.6 %collective-permute-start.8 = (bf16[256,640]{1,0:T(8,128)(2,1)S(1)}, bf16[256,640]{1,0:T(8,128)(2,1)S(1)}, u32[]{:S(2)}, u32[]{:S(2)}) collective-permute-start(bf16[256,640]{1,0:T(8,128)(2,1)S(1)} %copy-done.17), channel_id=1, source_target_pairs={{0,128},{8,136},{16,144},{24,152},{32,160},{40,168},{48,176},{56,1... | collective-permute-start | bytes 983048 | tf_op jit(solution)/shard_map/ppermute | solution.py:16
  67.5 33.5 %collective-permute-start.9 = (bf16[256,640]{1,0:T(8,128)(2,1)S(1)}, bf16[256,640]{1,0:T(8,128)(2,1)S(1)}, u32[]{:S(2)}, u32[]{:S(2)}) collective-permute-start(bf16[256,640]{1,0:T(8,128)(2,1)S(1)} %copy-done.17), channel_id=1, source_target_pairs={{128,0},{136,8},{144,16},{152,24},{160,32},{168,40},{176,48},{184,... | collective-permute-start | bytes 983048 | tf_op jit(solution)/shard_map/ppermute | solution.py:16
  70.6 57.8 %collective-permute-start.10 = (bf16[256,640]{1,0:T(8,128)(2,1)S(1)}, bf16[256,640]{1,0:T(8,128)(2,1)S(1)}, u32[]{:S(2)}, u32[]{:S(2)}) collective-permute-start(bf16[256,640]{1,0:T(8,128)(2,1)S(1)} %copy-done.18), channel_id=1, source_target_pairs={{0,8},{8,16},{16,24},{24,32},{32,40},{40,48},{48,56},{56,64},{64,7... | collective-permute-start | bytes 983048 | tf_op jit(solution)/shard_map/ppermute | solution.py:16
  87.3 43.8 %collective-permute-start.11 = (bf16[256,640]{1,0:T(8,128)(2,1)S(1)}, bf16[256,640]{1,0:T(8,128)(2,1)S(1)}, u32[]{:S(2)}, u32[]{:S(2)}) collective-permute-start(bf16[256,640]{1,0:T(8,128)(2,1)S(1)} %copy-done.18), channel_id=1, source_target_pairs={{8,0},{16,8},{24,16},{32,24},{40,32},{48,40},{56,48},{64,56},{72,6... | collective-permute-start | bytes 983048 | tf_op jit(solution)/shard_map/ppermute | solution.py:16
  90.0 46.1 %collective-permute-start.12 = (bf16[256,640]{1,0:T(8,128)(2,1)S(1)}, bf16[256,640]{1,0:T(8,128)(2,1)S(1)}, u32[]{:S(2)}, u32[]{:S(2)}) collective-permute-start(bf16[256,640]{1,0:T(8,128)(2,1)S(1)} %copy-done.18), channel_id=1, source_target_pairs={{0,16},{8,24},{16,32},{24,40},{32,48},{40,56},{48,64},{56,72},{64,... | collective-permute-start | bytes 983048 | tf_op jit(solution)/shard_map/ppermute | solution.py:16
  98.4 41.5 %collective-permute-start.13 = (bf16[256,640]{1,0:T(8,128)(2,1)S(1)}, bf16[256,640]{1,0:T(8,128)(2,1)S(1)}, u32[]{:S(2)}, u32[]{:S(2)}) collective-permute-start(bf16[256,640]{1,0:T(8,128)(2,1)S(1)} %copy-done.18), channel_id=1, source_target_pairs={{16,0},{24,8},{32,16},{40,24},{48,32},{56,40},{64,48},{72,56},{80,... | collective-permute-start | bytes 983048 | tf_op jit(solution)/shard_map/ppermute | solution.py:16
  101.0 46.2 %collective-permute-start.14 = (bf16[256,640]{1,0:T(8,128)(2,1)S(1)}, bf16[256,640]{1,0:T(8,128)(2,1)S(1)}, u32[]{:S(2)}, u32[]{:S(2)}) collective-permute-start(bf16[256,640]{1,0:T(8,128)(2,1)S(1)} %copy-done.18), channel_id=1, source_target_pairs={{0,32},{8,40},{16,48},{24,56},{32,64},{40,72},{48,80},{56,88},{64,... | collective-permute-start | bytes 983048 | tf_op jit(solution)/shard_map/ppermute | solution.py:16
  128.3 23.9 %collective-permute-start.15 = (bf16[256,640]{1,0:T(8,128)(2,1)S(1)}, bf16[256,640]{1,0:T(8,128)(2,1)S(1)}, u32[]{:S(2)}, u32[]{:S(2)}) collective-permute-start(bf16[256,640]{1,0:T(8,128)(2,1)S(1)} %copy-done.18), channel_id=1, source_target_pairs={{32,0},{40,8},{48,16},{56,24},{64,32},{72,40},{80,48},{88,56},{96,... | collective-permute-start | bytes 983048 | tf_op jit(solution)/shard_map/ppermute | solution.py:16
  131.0 25.8 %collective-permute-start.16 = (bf16[256,640]{1,0:T(8,128)(2,1)S(1)}, bf16[256,640]{1,0:T(8,128)(2,1)S(1)}, u32[]{:S(2)}, u32[]{:S(2)}) collective-permute-start(bf16[256,640]{1,0:T(8,128)(2,1)S(1)} %copy-done.18), channel_id=1, source_target_pairs={{0,64},{8,72},{16,80},{24,88},{32,96},{40,104},{48,112},{56,120},{... | collective-permute-start | bytes 983048 | tf_op jit(solution)/shard_map/ppermute | solution.py:16
  136.0 21.5 %collective-permute-start.17 = (bf16[256,640]{1,0:T(8,128)(2,1)S(1)}, bf16[256,640]{1,0:T(8,128)(2,1)S(1)}, u32[]{:S(2)}, u32[]{:S(2)}) collective-permute-start(bf16[256,640]{1,0:T(8,128)(2,1)S(1)} %copy-done.18), channel_id=1, source_target_pairs={{64,0},{72,8},{80,16},{88,24},{96,32},{104,40},{112,48},{120,56},{... | collective-permute-start | bytes 983048 | tf_op jit(solution)/shard_map/ppermute | solution.py:16
  139.9 28.3 %collective-permute-start.18 = (bf16[256,640]{1,0:T(8,128)(2,1)S(1)}, bf16[256,640]{1,0:T(8,128)(2,1)}, u32[]{:S(2)}, u32[]{:S(2)}) collective-permute-start(bf16[256,640]{1,0:T(8,128)(2,1)S(1)} %copy-done.18), channel_id=1, source_target_pairs={{0,128},{8,136},{16,144},{24,152},{32,160},{40,168},{48,176},{56,1... | collective-permute-start | bytes 983048 | tf_op jit(solution)/shard_map/ppermute | solution.py:16
  147.2 22.8 %collective-permute-start.19 = (bf16[256,640]{1,0:T(8,128)(2,1)S(1)}, bf16[256,640]{1,0:T(8,128)(2,1)}, u32[]{:S(2)}, u32[]{:S(2)}) collective-permute-start(bf16[256,640]{1,0:T(8,128)(2,1)S(1)} %copy-done.18), channel_id=1, source_target_pairs={{128,0},{136,8},{144,16},{152,24},{160,32},{168,40},{176,48},{184,... | collective-permute-start | bytes 983048 | tf_op jit(solution)/shard_map/ppermute | solution.py:16
  182.3 1.9 copy-start.2
  182.3 2.0 copy-start.4
  183.8 2.7 copy-start.21
  198.2 4.9 %copy-start.3 = (bf16[2,768,5,128]{3,2,1,0:T(8,128)(2,1)S(1)}, bf16[2,768,5,128]{3,2,1,0:T(8,128)(2,1)}, u32[]{:S(2)}) copy-start(bf16[2,768,5,128]{3,2,1,0:T(8,128)(2,1)} %reshape.144) | copy-start | bytes 5898244
  198.2 4.9 %copy-start.22 = (f32[2,5,128,768]{2,3,1,0:T(8,128)S(1)}, f32[2,5,128,768]{2,3,1,0:T(8,128)}, u32[]{:S(2)}) copy-start(f32[2,5,128,768]{2,3,1,0:T(8,128)} %copy-done.21) | copy-start | bytes 11796484
  204.0 1.3 copy-start
  229.2 53.8 %collective-permute-start.29 = (bf16[2,81920]{1,0:T(2,128)(2,1)}, bf16[2,81920]{1,0:T(2,128)(2,1)S(1)}, u32[]{:S(2)}, u32[]{:S(2)}) collective-permute-start(bf16[2,81920]{1,0:T(2,128)(2,1)} %get-tuple-element.29), channel_id=1, source_target_pairs={{0,128},{8,136},{16,144},{24,152},{32,160},{40,168},{48,176},{56,1... | collective-permute-start | bytes 983048 | tf_op jit(solution)/shard_map/ppermute | solution.py:16
  232.4 52.7 %collective-permute-start.28 = (bf16[2,81920]{1,0:T(2,128)(2,1)}, bf16[2,81920]{1,0:T(2,128)(2,1)S(1)}, u32[]{:S(2)}, u32[]{:S(2)}) collective-permute-start(bf16[2,81920]{1,0:T(2,128)(2,1)} %get-tuple-element.30), channel_id=1, source_target_pairs={{128,0},{136,8},{144,16},{152,24},{160,32},{168,40},{176,48},{184,... | collective-permute-start | bytes 983048 | tf_op jit(solution)/shard_map/ppermute | solution.py:16
  233.7 64.5 %collective-permute-start.27 = (bf16[2,81920]{1,0:T(2,128)(2,1)}, bf16[2,81920]{1,0:T(2,128)(2,1)S(1)}, u32[]{:S(2)}, u32[]{:S(2)}) collective-permute-start(bf16[2,81920]{1,0:T(2,128)(2,1)} %get-tuple-element.31), channel_id=1, source_target_pairs={{0,64},{8,72},{16,80},{24,88},{32,96},{40,104},{48,112},{56,120},{... | collective-permute-start | bytes 983048 | tf_op jit(solution)/shard_map/ppermute | solution.py:16
  249.8 50.2 %collective-permute-start.26 = (bf16[2,81920]{1,0:T(2,128)(2,1)}, bf16[2,81920]{1,0:T(2,128)(2,1)S(1)}, u32[]{:S(2)}, u32[]{:S(2)}) collective-permute-start(bf16[2,81920]{1,0:T(2,128)(2,1)} %get-tuple-element.32), channel_id=1, source_target_pairs={{64,0},{72,8},{80,16},{88,24},{96,32},{104,40},{112,48},{120,56},{... | collective-permute-start | bytes 983048 | tf_op jit(solution)/shard_map/ppermute | solution.py:16
  251.8 61.6 %collective-permute-start.25 = (bf16[2,81920]{1,0:T(2,128)(2,1)}, bf16[2,81920]{1,0:T(2,128)(2,1)}, u32[]{:S(2)}, u32[]{:S(2)}) collective-permute-start(bf16[2,81920]{1,0:T(2,128)(2,1)} %get-tuple-element.33), channel_id=1, source_target_pairs={{0,32},{8,40},{16,48},{24,56},{32,64},{40,72},{48,80},{56,88},{64,... | collective-permute-start | bytes 983048 | tf_op jit(solution)/shard_map/ppermute | solution.py:16
  273.8 9.1 %copy-start.15 = (bf16[2,81920]{1,0:T(2,128)(2,1)S(1)}, bf16[2,81920]{1,0:T(2,128)(2,1)}, u32[]{:S(2)}) copy-start(bf16[2,81920]{1,0:T(2,128)(2,1)} %get-tuple-element.34) | copy-start | bytes 983044
  273.8 11.2 %copy-start.14 = (bf16[2,81920]{1,0:T(2,128)(2,1)S(1)}, bf16[2,81920]{1,0:T(2,128)(2,1)}, u32[]{:S(2)}) copy-start(bf16[2,81920]{1,0:T(2,128)(2,1)} %get-tuple-element.35) | copy-start | bytes 983044
  273.9 24.3 %copy-start.13 = (bf16[2,81920]{1,0:T(2,128)(2,1)S(1)}, bf16[2,81920]{1,0:T(2,128)(2,1)}, u32[]{:S(2)}) copy-start(bf16[2,81920]{1,0:T(2,128)(2,1)} %get-tuple-element.36) | copy-start | bytes 983044
  273.9 26.2 %copy-start.12 = (bf16[2,81920]{1,0:T(2,128)(2,1)S(1)}, bf16[2,81920]{1,0:T(2,128)(2,1)}, u32[]{:S(2)}) copy-start(bf16[2,81920]{1,0:T(2,128)(2,1)} %get-tuple-element.37) | copy-start | bytes 983044
  273.9 39.5 %copy-start.10 = (bf16[2,81920]{1,0:T(2,128)(2,1)S(1)}, bf16[2,81920]{1,0:T(2,128)(2,1)}, u32[]{:S(2)}) copy-start(bf16[2,81920]{1,0:T(2,128)(2,1)} %get-tuple-element.28) | copy-start | bytes 983044
  283.0 61.0 %copy-start.1 = (bf16[2,5,128,768]{2,3,1,0:T(8,128)(2,1)S(1)}, bf16[2,5,128,768]{2,3,1,0:T(8,128)(2,1)}, u32[]{:S(2)}) copy-start(bf16[2,5,128,768]{2,3,1,0:T(8,128)(2,1)} %copy-done) | copy-start | bytes 5898244
  283.0 36.2 %collective-permute-start.24 = (bf16[2,81920]{1,0:T(2,128)(2,1)S(1)}, bf16[2,81920]{1,0:T(2,128)(2,1)S(1)}, u32[]{:S(2)}, u32[]{:S(2)}) collective-permute-start(bf16[2,81920]{1,0:T(2,128)(2,1)S(1)} %copy-done.15), channel_id=1, source_target_pairs={{32,0},{40,8},{48,16},{56,24},{64,32},{72,40},{80,48},{88,56},{96,... | collective-permute-start | bytes 983048 | tf_op jit(solution)/shard_map/ppermute | solution.py:16
  285.1 36.1 %collective-permute-start.23 = (bf16[2,81920]{1,0:T(2,128)(2,1)S(1)}, bf16[2,81920]{1,0:T(2,128)(2,1)S(1)}, u32[]{:S(2)}, u32[]{:S(2)}) collective-permute-start(bf16[2,81920]{1,0:T(2,128)(2,1)S(1)} %copy-done.14), channel_id=1, source_target_pairs={{0,16},{8,24},{16,32},{24,40},{32,48},{40,56},{48,64},{56,72},{64,... | collective-permute-start | bytes 983048 | tf_op jit(solution)/shard_map/ppermute | solution.py:16
  298.1 25.2 %collective-permute-start.22 = (bf16[2,81920]{1,0:T(2,128)(2,1)S(1)}, bf16[2,81920]{1,0:T(2,128)(2,1)S(1)}, u32[]{:S(2)}, u32[]{:S(2)}) collective-permute-start(bf16[2,81920]{1,0:T(2,128)(2,1)S(1)} %copy-done.13), channel_id=1, source_target_pairs={{16,0},{24,8},{32,16},{40,24},{48,32},{56,40},{64,48},{72,56},{80,... | collective-permute-start | bytes 983048 | tf_op jit(solution)/shard_map/ppermute | solution.py:16
  300.1 41.9 %copy-start.5 = (bf16[2,81920]{1,0:T(2,128)(2,1)}, bf16[2,81920]{1,0:T(2,128)(2,1)S(1)}, u32[]{:S(2)}) copy-start(bf16[2,81920]{1,0:T(2,128)(2,1)S(1)} %collective-permute-done.26) | copy-start | bytes 983044
  300.1 40.0 %collective-permute-start.21 = (bf16[2,81920]{1,0:T(2,128)(2,1)S(1)}, bf16[2,81920]{1,0:T(2,128)(2,1)S(1)}, u32[]{:S(2)}, u32[]{:S(2)}) collective-permute-start(bf16[2,81920]{1,0:T(2,128)(2,1)S(1)} %copy-done.12), channel_id=1, source_target_pairs={{0,8},{8,16},{16,24},{24,32},{32,40},{40,48},{48,56},{56,64},{64,7... | collective-permute-start | bytes 983048 | tf_op jit(solution)/shard_map/ppermute | solution.py:16
  313.4 28.6 %collective-permute-start.20 = (bf16[2,81920]{1,0:T(2,128)(2,1)S(1)}, bf16[2,81920]{1,0:T(2,128)(2,1)S(1)}, u32[]{:S(2)}, u32[]{:S(2)}) collective-permute-start(bf16[2,81920]{1,0:T(2,128)(2,1)S(1)} %copy-done.10), channel_id=1, source_target_pairs={{8,0},{16,8},{24,16},{32,24},{40,32},{48,40},{56,48},{64,56},{72,6... | collective-permute-start | bytes 983048 | tf_op jit(solution)/shard_map/ppermute | solution.py:16
  319.1 24.8 %copy-start.6 = (bf16[2,81920]{1,0:T(2,128)(2,1)}, bf16[2,81920]{1,0:T(2,128)(2,1)S(1)}, u32[]{:S(2)}) copy-start(bf16[2,81920]{1,0:T(2,128)(2,1)S(1)} %collective-permute-done.24) | copy-start | bytes 983044
  319.2 35.7 %collective-permute-start.39 = (bf16[2,81920]{1,0:T(2,128)(2,1)}, bf16[2,81920]{1,0:T(2,128)(2,1)}, u32[]{:S(2)}, u32[]{:S(2)}) collective-permute-start(bf16[2,81920]{1,0:T(2,128)(2,1)} %get-tuple-element.19), channel_id=1, source_target_pairs={{0,128},{8,136},{16,144},{24,152},{32,160},{40,168},{48,176},{56,1... | collective-permute-start | bytes 983048 | tf_op jit(solution)/shard_map/ppermute | solution.py:16
  321.2 22.8 %copy-start.7 = (bf16[2,81920]{1,0:T(2,128)(2,1)}, bf16[2,81920]{1,0:T(2,128)(2,1)S(1)}, u32[]{:S(2)}) copy-start(bf16[2,81920]{1,0:T(2,128)(2,1)S(1)} %collective-permute-done.23) | copy-start | bytes 983044
  321.2 35.6 %collective-permute-start.38 = (bf16[2,81920]{1,0:T(2,128)(2,1)}, bf16[2,81920]{1,0:T(2,128)(2,1)}, u32[]{:S(2)}, u32[]{:S(2)}) collective-permute-start(bf16[2,81920]{1,0:T(2,128)(2,1)} %get-tuple-element.20), channel_id=1, source_target_pairs={{128,0},{136,8},{144,16},{152,24},{160,32},{168,40},{176,48},{184,... | collective-permute-start | bytes 983048 | tf_op jit(solution)/shard_map/ppermute | solution.py:16
  323.4 20.6 %copy-start.8 = (bf16[2,81920]{1,0:T(2,128)(2,1)}, bf16[2,81920]{1,0:T(2,128)(2,1)S(1)}, u32[]{:S(2)}) copy-start(bf16[2,81920]{1,0:T(2,128)(2,1)S(1)} %collective-permute-done.22) | copy-start | bytes 983044
  323.4 45.5 %collective-permute-start.37 = (bf16[2,81920]{1,0:T(2,128)(2,1)}, bf16[2,81920]{1,0:T(2,128)(2,1)}, u32[]{:S(2)}, u32[]{:S(2)}) collective-permute-start(bf16[2,81920]{1,0:T(2,128)(2,1)} %get-tuple-element.21), channel_id=1, source_target_pairs={{0,64},{8,72},{16,80},{24,88},{32,96},{40,104},{48,112},{56,120},{... | collective-permute-start | bytes 983048 | tf_op jit(solution)/shard_map/ppermute | solution.py:16
  340.1 3.9 copy-start.9
  340.1 30.7 %collective-permute-start.36 = (bf16[2,81920]{1,0:T(2,128)(2,1)}, bf16[2,81920]{1,0:T(2,128)(2,1)}, u32[]{:S(2)}, u32[]{:S(2)}) collective-permute-start(bf16[2,81920]{1,0:T(2,128)(2,1)} %get-tuple-element.22), channel_id=1, source_target_pairs={{64,0},{72,8},{80,16},{88,24},{96,32},{104,40},{112,48},{120,56},{... | collective-permute-start | bytes 983048 | tf_op jit(solution)/shard_map/ppermute | solution.py:16
  342.0 2.0 copy-start.11
  342.0 40.7 %collective-permute-start.35 = (bf16[2,81920]{1,0:T(2,128)(2,1)}, bf16[2,81920]{1,0:T(2,128)(2,1)}, u32[]{:S(2)}, u32[]{:S(2)}) collective-permute-start(bf16[2,81920]{1,0:T(2,128)(2,1)} %get-tuple-element.23), channel_id=1, source_target_pairs={{0,32},{8,40},{16,48},{24,56},{32,64},{40,72},{48,80},{56,88},{64,... | collective-permute-start | bytes 983048 | tf_op jit(solution)/shard_map/ppermute | solution.py:16
  354.9 35.2 %collective-permute-start.34 = (bf16[2,81920]{1,0:T(2,128)(2,1)}, bf16[2,81920]{1,0:T(2,128)(2,1)S(1)}, u32[]{:S(2)}, u32[]{:S(2)}) collective-permute-start(bf16[2,81920]{1,0:T(2,128)(2,1)} %get-tuple-element.24), channel_id=1, source_target_pairs={{32,0},{40,8},{48,16},{56,24},{64,32},{72,40},{80,48},{88,56},{96,... | collective-permute-start | bytes 983048 | tf_op jit(solution)/shard_map/ppermute | solution.py:16
  356.8 33.2 %collective-permute-start.33 = (bf16[2,81920]{1,0:T(2,128)(2,1)}, bf16[2,81920]{1,0:T(2,128)(2,1)S(1)}, u32[]{:S(2)}, u32[]{:S(2)}) collective-permute-start(bf16[2,81920]{1,0:T(2,128)(2,1)} %get-tuple-element.25), channel_id=1, source_target_pairs={{0,16},{8,24},{16,32},{24,40},{32,48},{40,56},{48,64},{56,72},{64,... | collective-permute-start | bytes 983048 | tf_op jit(solution)/shard_map/ppermute | solution.py:16
  368.9 21.1 %collective-permute-start.32 = (bf16[2,81920]{1,0:T(2,128)(2,1)}, bf16[2,81920]{1,0:T(2,128)(2,1)S(1)}, u32[]{:S(2)}, u32[]{:S(2)}) collective-permute-start(bf16[2,81920]{1,0:T(2,128)(2,1)} %get-tuple-element.26), channel_id=1, source_target_pairs={{16,0},{24,8},{32,16},{40,24},{48,32},{56,40},{64,48},{72,56},{80,... | collective-permute-start | bytes 983048 | tf_op jit(solution)/shard_map/ppermute | solution.py:16
  370.8 24.7 %collective-permute-start.31 = (bf16[2,81920]{1,0:T(2,128)(2,1)}, bf16[2,81920]{1,0:T(2,128)(2,1)S(1)}, u32[]{:S(2)}, u32[]{:S(2)}) collective-permute-start(bf16[2,81920]{1,0:T(2,128)(2,1)} %get-tuple-element.27), channel_id=1, source_target_pairs={{0,8},{8,16},{16,24},{24,32},{32,40},{40,48},{48,56},{56,64},{64,7... | collective-permute-start | bytes 983048 | tf_op jit(solution)/shard_map/ppermute | solution.py:16
  382.8 28.0 %collective-permute-start.30 = (bf16[2,81920]{1,0:T(2,128)(2,1)}, bf16[2,81920]{1,0:T(2,128)(2,1)S(1)}, u32[]{:S(2)}, u32[]{:S(2)}) collective-permute-start(bf16[2,81920]{1,0:T(2,128)(2,1)} %get-tuple-element.18), channel_id=1, source_target_pairs={{8,0},{16,8},{24,16},{32,24},{40,32},{48,40},{56,48},{64,56},{72,6... | collective-permute-start | bytes 983048 | tf_op jit(solution)/shard_map/ppermute | solution.py:16
where the time goes:
time: 418 us; the launch traced here: 416 us
  starting transfers between devices  164 us (39%)
  waiting for transfers between devices  117 us (28%)
  local copies, waits for them, and re-layouts  82.9 us (20%)
  matrix products  28 us (7%)
  other arithmetic  12 us (3%)
  blocking collectives  10.3 us (2%)
    ppermute x40, starting transfers between devices, from_behind(): lax.ppermute(value, axis, [(source, source + steps) for source in range(l...  164 us
    ppermute x40, waiting for transfers between devices, from_behind(): lax.ppermute(value, axis, [(source, source + steps) for source in range(l...  117 us
    unnamed x70, local copies, waits for them, and re-layouts  25.8 us
    psum x1, blocking collectives, local(): squares = lax.psum(jnp.sum(diff * diff, axis=(2, 3)), 'head')  10.3 us
    dot_general x1, matrix products, local(): jnp.dot(selector, part_v, precision=lax.Precision.HIGHEST)  9.11 us
    dot_general x1, matrix products, local(): jnp.dot(selector, part_k, precision=lax.Precision.HIGHEST)  9 us
  transfers between devices with their start and end apart: 40, of which 15 were waited for; matrix products, arithmetic and copies ran while one was open for 17% of the time, Pallas kernels for 0%

commit v1 on v0

--- a/solution.py
+++ b/solution.py
@@ -62,7 +62,7 @@
     probs16 = probs.astype(jnp.bfloat16)
     attn = jnp.einsum("bhqk,bkhd->bqhd", probs16, value_block, preferred_element_type=jnp.float32)
     diff = attn - ref_velocity.reshape(blocks_here, BLK, heads_here, HD).astype(jnp.float32)
-    squares = lax.psum(jnp.sum(diff * diff, axis=(2, 3)), "head")
+    squares = jnp.sum(lax.all_gather(jnp.sum(diff * diff, axis=(2, 3)), "head"), axis=0)
     kl = squares / (HEADS * HD)
     upstream = (
         policy_grad.reshape(blocks_here, BLK, heads_here, HD).astype(jnp.float32)

time: 418 us -> 416 us (level)
    psum x1 -> x0, blocking collectives: 10.3 us -> none  [local(): squares = lax.psum(jnp.sum(diff * diff, axis=(2, 3)), 'head')]
    all_gather x0 -> x1, blocking collectives: none -> 9.58 us  [local(): lax.all_gather(jnp.sum(diff * diff, axis=(2, 3)), 'head')]
    ppermute x40, starting transfers between devices: 164 us -> 160 us  [from_behind(): lax.ppermute(value, axis, [(source, source + steps) for source in range(l...]
  transfers between devices with their start and end apart: 40 -> 40, of which waited for: 15 -> 17; matrix products, arithmetic and copies ran while one was open for 17% -> 17% of each run, Pallas kernels for 0% -> 0%
where the time goes in v1:
time: 416 us; the launch traced here: 413 us
  starting transfers between devices  160 us (38%)
  waiting for transfers between devices  119 us (29%)
  local copies, waits for them, and re-layouts  82.9 us (20%)
  matrix products  28 us (7%)
  other arithmetic  12.1 us (3%)
  blocking collectives  9.58 us (2%)
    ppermute x40, starting transfers between devices, from_behind(): lax.ppermute(value, axis, [(source, source + steps) for source in range(l...  160 us
    ppermute x40, waiting for transfers between devices, from_behind(): lax.ppermute(value, axis, [(source, source + steps) for source in range(l...  119 us
    unnamed x70, local copies, waits for them, and re-layouts  25.8 us
    all_gather x1, blocking collectives, local(): lax.all_gather(jnp.sum(diff * diff, axis=(2, 3)), 'head')  9.58 us
    dot_general x1, matrix products, local(): jnp.dot(selector, part_v, precision=lax.Precision.HIGHEST)  9.11 us
    dot_general x1, matrix products, local(): jnp.dot(selector, part_k, precision=lax.Precision.HIGHEST)  9 us
  transfers between devices with their start and end apart: 40, of which 17 were waited for; matrix products, arithmetic and copies ran while one was open for 17% of the time, Pallas kernels for 0%

profile of v1, /device:TPU:94, one launch (start us, length us, event | category | flops | bytes accessed | tf_op | source)
XLA Modules:
  0.0 413.0 jit_solution(15818609672130254806)
XLA Ops:
  0.7 7.0 %collective-permute-start = (bf16[256,640]{1,0:T(8,128)(2,1)}, bf16[256,640]{1,0:T(8,128)(2,1)}, u32[]{:S(2)}, u32[]{:S(2)}) collective-permute-start(bf16[256,640]{1,0:T(8,128)(2,1)} %param.8), channel_id=1, source_target_pairs={{0,8},{8,16},{16,24},{24,32},{32,40},{40,48},{48,56},{56,64},{64,7... | collective-permute-start | bytes 983048 | tf_op jit(solution)/shard_map/ppermute | solution.py:16
  7.7 1.9 collective-permute-start.1
  9.6 4.9 %collective-permute-start.2 = (bf16[256,640]{1,0:T(8,128)(2,1)}, bf16[256,640]{1,0:T(8,128)(2,1)}, u32[]{:S(2)}, u32[]{:S(2)}) collective-permute-start(bf16[256,640]{1,0:T(8,128)(2,1)} %param.8), channel_id=1, source_target_pairs={{0,16},{8,24},{16,32},{24,40},{32,48},{40,56},{48,64},{56,72},{64,... | collective-permute-start | bytes 983048 | tf_op jit(solution)/shard_map/ppermute | solution.py:16
  14.5 2.5 collective-permute-start.3
  17.0 4.0 collective-permute-start.4
  29.1 8.1 %collective-permute-done = bf16[256,640]{1,0:T(8,128)(2,1)} collective-permute-done((bf16[256,640]{1,0:T(8,128)(2,1)}, bf16[256,640]{1,0:T(8,128)(2,1)}, u32[]{:S(2)}, u32[]{:S(2)}) %collective-permute-start) | collective-permute-done | bytes 327712 | tf_op jit(solution)/shard_map/ppermute | solution.py:16
  37.1 1.9 collective-permute-start.5
  40.8 2.2 collective-permute-done.1
  43.0 1.9 collective-permute-start.6
  46.7 11.4 %collective-permute-done.2 = bf16[256,640]{1,0:T(8,128)(2,1)} collective-permute-done((bf16[256,640]{1,0:T(8,128)(2,1)}, bf16[256,640]{1,0:T(8,128)(2,1)}, u32[]{:S(2)}, u32[]{:S(2)}) %collective-permute-start.2) | collective-permute-done | bytes 327712 | tf_op jit(solution)/shard_map/ppermute | solution.py:16
  58.1 1.9 collective-permute-start.7
  64.8 2.8 collective-permute-done.4
  70.6 15.9 %collective-permute-start.10 = (bf16[256,640]{1,0:T(8,128)(2,1)S(1)}, bf16[256,640]{1,0:T(8,128)(2,1)S(1)}, u32[]{:S(2)}, u32[]{:S(2)}) collective-permute-start(bf16[256,640]{1,0:T(8,128)(2,1)S(1)} %copy-done.18), channel_id=1, source_target_pairs={{0,8},{8,16},{16,24},{24,32},{32,40},{40,48},{48,56},{56,64},{64,7... | collective-permute-start | bytes 983048 | tf_op jit(solution)/shard_map/ppermute | solution.py:16
  87.3 1.9 collective-permute-start.11
  90.0 7.6 %collective-permute-start.12 = (bf16[256,640]{1,0:T(8,128)(2,1)S(1)}, bf16[256,640]{1,0:T(8,128)(2,1)S(1)}, u32[]{:S(2)}, u32[]{:S(2)}) collective-permute-start(bf16[256,640]{1,0:T(8,128)(2,1)S(1)} %copy-done.18), channel_id=1, source_target_pairs={{0,16},{8,24},{16,32},{24,40},{32,48},{40,56},{48,64},{56,72},{64,... | collective-permute-start | bytes 983048 | tf_op jit(solution)/shard_map/ppermute | solution.py:16
  98.4 1.9 collective-permute-start.13
  101.0 2.5 collective-permute-start.14
  104.3 24.1 %collective-permute-done.10 = bf16[256,640]{1,0:T(8,128)(2,1)S(1)} collective-permute-done((bf16[256,640]{1,0:T(8,128)(2,1)S(1)}, bf16[256,640]{1,0:T(8,128)(2,1)S(1)}, u32[]{:S(2)}, u32[]{:S(2)}) %collective-permute-start.10) | collective-permute-done | bytes 327712 | tf_op jit(solution)/shard_map/ppermute | solution.py:16
  128.3 1.9 collective-permute-start.15
  131.0 1.9 collective-permute-start.16
  133.7 2.3 collective-permute-done.12
  136.0 3.1 collective-permute-start.17
  139.9 2.0 collective-permute-start.18
  142.7 4.5 %collective-permute-done.14 = bf16[256,640]{1,0:T(8,128)(2,1)S(1)} collective-permute-done((bf16[256,640]{1,0:T(8,128)(2,1)S(1)}, bf16[256,640]{1,0:T(8,128)(2,1)S(1)}, u32[]{:S(2)}, u32[]{:S(2)}) %collective-permute-start.14) | collective-permute-done | bytes 327712 | tf_op jit(solution)/shard_map/ppermute | solution.py:16
  149.2 3.0 collective-permute-done.15
  153.0 3.8 collective-permute-done.16
  158.3 2.9 gather_fusion
  161.3 3.5 reshape.150
  164.8 3.5 copy.99
  171.7 4.3 %gather_fusion.1 = bf16[12,128,640]{2,1,0:T(8,128)(2,1)} fusion(bf16[22,128,640]{2,1,0:T(8,128)(2,1)} %bitcast.87, s32[1024]{0:T(1024)S(1)} %pad_clamp_fusion), kind=kCustom, calls=%fused_computation.1 | custom fusion | bytes 3932208 | tf_op jit(solution)/shard_map/gather | solution.py:46
  175.9 5.6 %reshape.151 = bf16[2,768,5,128]{3,2,1,0:T(8,128)(2,1)} reshape(bf16[12,128,640]{2,1,0:T(8,128)(2,1)} %gather_fusion.1) | data formatting | bytes 3932160 | tf_op jit(solution)/shard_map/reshape | solution.py:46
  184.3 2.1 multiply_reduce_fusion.1
  186.5 9.6 %all-gather.1 = f32[8,2,128]{2,1,0:T(2,128)S(1)} all-gather(f32[1,2,128]{2,1,0:T(2,128)S(1)} %bitcast.91), channel_id=2, replica_groups=mesh['frame'=32,'head'=8] {'head'}, dimensions={0}, use_global_device_ids=true | all-gather | bytes 9216 | tf_op jit(solution)/shard_map/all_gather | solution.py:65
  197.5 4.9 %convolution_bitcast_fusion = f32[2,768,5,128]{1,3,2,0:T(8,128)} fusion(bf16[2,128,5,128]{1,3,2,0:T(8,128)(2,1)S(1)} %get-tuple-element.16, f32[2,5,128,768]{2,3,1,0:T(8,128)} %copy-done.21, f32[2,5,128]{2,1,0:T(8,128)S(1)} %get-tuple-element.41), kind=kOutput, calls=%fused_computation.10 | convolution fusion | flops 253624320 | bytes 8197120 | tf_op jit(solution)/shard_map/bhqk,bqhd->bkhd/dot_general | solution.py:85
  205.3 5.0 %copy.103 = f32[2,768,5,128]{3,2,1,0:T(8,128)} copy(f32[2,768,5,128]{3,1,2,0:T(8,128)S(1)} %multiply_bitcast_fusion) | data formatting | bytes 7864320 | tf_op jit(solution)/shard_map/mul | solution.py:82
  210.3 5.4 %reshape.116 = f32[12,81920]{1,0:T(8,128)} reshape(f32[2,768,5,128]{3,2,1,0:T(8,128)} %copy.103) | data formatting | bytes 7864320 | tf_op jit(solution)/shard_map/reshape | solution.py:86
  215.7 9.0 %fusion.48 = (bf16[22,81920]{1,0:T(8,128)(2,1)S(1)}, f32[22,81920]{1,0:T(8,128)}) fusion(f32[12,81920]{1,0:T(8,128)} %reshape.116, s32[12]{0:T(128)S(1)} %eq.75), kind=kOutput, calls=%fused_computation.109 | convolution fusion | flops 261325056 | bytes 14745648 | tf_op jit(solution)/shard_map/dot_general | solution.py:92
  224.7 3.8 fusion.46
  231.1 15.7 %collective-permute-start.27 = (bf16[2,81920]{1,0:T(2,128)(2,1)}, bf16[2,81920]{1,0:T(2,128)(2,1)S(1)}, u32[]{:S(2)}, u32[]{:S(2)}) collective-permute-start(bf16[2,81920]{1,0:T(2,128)(2,1)} %get-tuple-element.34), channel_id=1, source_target_pairs={{0,64},{8,72},{16,80},{24,88},{32,96},{40,104},{48,112},{56,120},{... | collective-permute-start | bytes 983048 | tf_op jit(solution)/shard_map/ppermute | solution.py:16
  246.7 1.9 collective-permute-start.26
  248.7 11.5 %collective-permute-start.25 = (bf16[2,81920]{1,0:T(2,128)(2,1)}, bf16[2,81920]{1,0:T(2,128)(2,1)}, u32[]{:S(2)}, u32[]{:S(2)}) collective-permute-start(bf16[2,81920]{1,0:T(2,128)(2,1)} %get-tuple-element.36), channel_id=1, source_target_pairs={{0,32},{8,40},{16,48},{24,56},{32,64},{40,72},{48,80},{56,88},{64,... | collective-permute-start | bytes 983048 | tf_op jit(solution)/shard_map/ppermute | solution.py:16
  260.2 6.0 %copy.105 = f32[2,768,5,128]{3,2,1,0:T(8,128)} copy(f32[2,768,5,128]{1,3,2,0:T(8,128)} %convolution_bitcast_fusion) | data formatting | bytes 7864320 | tf_op jit(solution)/shard_map/bhqk,bqhd->bkhd/transpose | solution.py:85
  266.2 5.3 %reshape.117 = f32[12,81920]{1,0:T(8,128)} reshape(f32[2,768,5,128]{3,2,1,0:T(8,128)} %copy.105) | data formatting | bytes 7864320 | tf_op jit(solution)/shard_map/reshape | solution.py:87
  271.5 9.1 %fusion.49 = (bf16[22,81920]{1,0:T(8,128)(2,1)S(1)}, f32[22,81920]{1,0:T(8,128)}) fusion(f32[12,81920]{1,0:T(8,128)} %reshape.117, s32[12]{0:T(128)S(1)} %eq.75), kind=kOutput, calls=%fused_computation.110 | convolution fusion | flops 261325056 | bytes 14745648 | tf_op jit(solution)/shard_map/dot_general | solution.py:95
  280.6 2.1 collective-permute-start.24
  282.7 13.0 %collective-permute-start.23 = (bf16[2,81920]{1,0:T(2,128)(2,1)S(1)}, bf16[2,81920]{1,0:T(2,128)(2,1)S(1)}, u32[]{:S(2)}, u32[]{:S(2)}) collective-permute-start(bf16[2,81920]{1,0:T(2,128)(2,1)S(1)} %copy-done.14), channel_id=1, source_target_pairs={{0,16},{8,24},{16,32},{24,40},{32,48},{40,56},{48,64},{56,72},{64,... | collective-permute-start | bytes 983048 | tf_op jit(solution)/shard_map/ppermute | solution.py:16
  295.7 1.9 collective-permute-start.22
  297.7 13.4 %collective-permute-start.21 = (bf16[2,81920]{1,0:T(2,128)(2,1)S(1)}, bf16[2,81920]{1,0:T(2,128)(2,1)S(1)}, u32[]{:S(2)}, u32[]{:S(2)}) collective-permute-start(bf16[2,81920]{1,0:T(2,128)(2,1)S(1)} %copy-done.12), channel_id=1, source_target_pairs={{0,8},{8,16},{16,24},{24,32},{32,40},{40,48},{48,56},{56,64},{64,7... | collective-permute-start | bytes 983048 | tf_op jit(solution)/shard_map/ppermute | solution.py:16
  311.0 1.9 collective-permute-start.20
  313.0 3.8 fusion.45
  316.8 2.0 collective-permute-start.39
  321.3 1.9 collective-permute-start.37
  323.2 12.5 %collective-permute-done.21 = bf16[2,81920]{1,0:T(2,128)(2,1)S(1)} collective-permute-done((bf16[2,81920]{1,0:T(2,128)(2,1)S(1)}, bf16[2,81920]{1,0:T(2,128)(2,1)S(1)}, u32[]{:S(2)}, u32[]{:S(2)}) %collective-permute-start.21) | collective-permute-done | bytes 327712 | tf_op jit(solution)/shard_map/ppermute | solution.py:16
  335.7 1.9 collective-permute-start.36
  338.2 1.9 collective-permute-start.35
  341.9 12.3 %collective-permute-done.39 = bf16[2,81920]{1,0:T(2,128)(2,1)} collective-permute-done((bf16[2,81920]{1,0:T(2,128)(2,1)}, bf16[2,81920]{1,0:T(2,128)(2,1)}, u32[]{:S(2)}, u32[]{:S(2)}) %collective-permute-start.39) | collective-permute-done | bytes 327712 | tf_op jit(solution)/shard_map/ppermute | solution.py:16
  356.2 1.9 collective-permute-start.33
  358.1 10.2 %collective-permute-done.37 = bf16[2,81920]{1,0:T(2,128)(2,1)} collective-permute-done((bf16[2,81920]{1,0:T(2,128)(2,1)}, bf16[2,81920]{1,0:T(2,128)(2,1)}, u32[]{:S(2)}, u32[]{:S(2)}) %collective-permute-start.37) | collective-permute-done | bytes 327712 | tf_op jit(solution)/shard_map/ppermute | solution.py:16
  370.2 10.1 %collective-permute-start.31 = (bf16[2,81920]{1,0:T(2,128)(2,1)}, bf16[2,81920]{1,0:T(2,128)(2,1)S(1)}, u32[]{:S(2)}, u32[]{:S(2)}) collective-permute-start(bf16[2,81920]{1,0:T(2,128)(2,1)} %get-tuple-element.30), channel_id=1, source_target_pairs={{0,8},{8,16},{16,24},{24,32},{32,40},{40,48},{48,56},{56,64},{64,7... | collective-permute-start | bytes 983048 | tf_op jit(solution)/shard_map/ppermute | solution.py:16
  380.3 2.2 collective-permute-start.30
  382.5 4.1 %add_convert_fusion.1 = bf16[2,81920]{1,0:T(2,128)(2,1)S(1)} fusion(bf16[2,81920]{1,0:T(2,128)(2,1)S(1)} %collective-permute-done.29, bf16[2,81920]{1,0:T(2,128)(2,1)S(1)} %collective-permute-done.28, bf16[2,81920]{1,0:T(2,128)(2,1)S(1)} %collective-permute-done.27, bf16[2,81920]{1,0:T(2,128)(2,1)} %copy-done.5, ...), kind=kLoop, calls=%fused_computation.35 | loop fusion | flops 3440640 | bytes 4259840 | tf_op jit(solution)/shard_map/convert_element_type | solution.py:109
  389.4 4.2 %collective-permute-done.31 = bf16[2,81920]{1,0:T(2,128)(2,1)S(1)} collective-permute-done((bf16[2,81920]{1,0:T(2,128)(2,1)}, bf16[2,81920]{1,0:T(2,128)(2,1)S(1)}, u32[]{:S(2)}, u32[]{:S(2)}) %collective-permute-start.31) | collective-permute-done | bytes 327712 | tf_op jit(solution)/shard_map/ppermute | solution.py:16
  393.6 14.5 %collective-permute-done.30 = bf16[2,81920]{1,0:T(2,128)(2,1)S(1)} collective-permute-done((bf16[2,81920]{1,0:T(2,128)(2,1)}, bf16[2,81920]{1,0:T(2,128)(2,1)S(1)}, u32[]{:S(2)}, u32[]{:S(2)}) %collective-permute-start.30) | collective-permute-done | bytes 327712 | tf_op jit(solution)/shard_map/ppermute | solution.py:16
  408.0 4.0 add_convert_fusion
  (129 shorter events, 55.8 us)
Async XLA Ops:
  0.6 26.1 %copy-start.18 = (bf16[256,640]{1,0:T(8,128)(2,1)S(1)}, bf16[256,640]{1,0:T(8,128)(2,1)}, u32[]{:S(2)}) copy-start(bf16[256,640]{1,0:T(8,128)(2,1)} %param.9) | copy-start | bytes 983044
  0.6 26.9 %copy-start.16 = (bf16[256,640]{1,0:T(8,128)(2,1)S(1)}, bf16[256,640]{1,0:T(8,128)(2,1)}, u32[]{:S(2)}) copy-start(bf16[256,640]{1,0:T(8,128)(2,1)} %param.7) | copy-start | bytes 983044
  0.7 27.3 %copy-start.20 = (s32[64]{0:T(128)S(1)}, s32[64]{0:T(128)}, u32[]{:S(2)}) copy-start(s32[64]{0:T(128)} %param.13) | copy-start | bytes 772
  0.7 27.7 %copy-start.19 = (bf16[256,640]{1,0:T(8,128)(2,1)S(1)}, bf16[256,640]{1,0:T(8,128)(2,1)}, u32[]{:S(2)}) copy-start(bf16[256,640]{1,0:T(8,128)(2,1)} %param.10) | copy-start | bytes 983044
  0.7 36.5 %collective-permute-start = (bf16[256,640]{1,0:T(8,128)(2,1)}, bf16[256,640]{1,0:T(8,128)(2,1)}, u32[]{:S(2)}, u32[]{:S(2)}) collective-permute-start(bf16[256,640]{1,0:T(8,128)(2,1)} %param.8), channel_id=1, source_target_pairs={{0,8},{8,16},{16,24},{24,32},{32,40},{40,48},{48,56},{56,64},{64,7... | collective-permute-start | bytes 983048 | tf_op jit(solution)/shard_map/ppermute | solution.py:16
  7.7 35.3 %collective-permute-start.1 = (bf16[256,640]{1,0:T(8,128)(2,1)}, bf16[256,640]{1,0:T(8,128)(2,1)}, u32[]{:S(2)}, u32[]{:S(2)}) collective-permute-start(bf16[256,640]{1,0:T(8,128)(2,1)} %param.8), channel_id=1, source_target_pairs={{8,0},{16,8},{24,16},{32,24},{40,32},{48,40},{56,48},{64,56},{72,6... | collective-permute-start | bytes 983048 | tf_op jit(solution)/shard_map/ppermute | solution.py:16
  9.6 48.4 %collective-permute-start.2 = (bf16[256,640]{1,0:T(8,128)(2,1)}, bf16[256,640]{1,0:T(8,128)(2,1)}, u32[]{:S(2)}, u32[]{:S(2)}) collective-permute-start(bf16[256,640]{1,0:T(8,128)(2,1)} %param.8), channel_id=1, source_target_pairs={{0,16},{8,24},{16,32},{24,40},{32,48},{40,56},{48,64},{56,72},{64,... | collective-permute-start | bytes 983048 | tf_op jit(solution)/shard_map/ppermute | solution.py:16
  14.5 47.3 %collective-permute-start.3 = (bf16[256,640]{1,0:T(8,128)(2,1)}, bf16[256,640]{1,0:T(8,128)(2,1)}, u32[]{:S(2)}, u32[]{:S(2)}) collective-permute-start(bf16[256,640]{1,0:T(8,128)(2,1)} %param.8), channel_id=1, source_target_pairs={{16,0},{24,8},{32,16},{40,24},{48,32},{56,40},{64,48},{72,56},{80,... | collective-permute-start | bytes 983048 | tf_op jit(solution)/shard_map/ppermute | solution.py:16
  17.0 50.6 %collective-permute-start.4 = (bf16[256,640]{1,0:T(8,128)(2,1)}, bf16[256,640]{1,0:T(8,128)(2,1)}, u32[]{:S(2)}, u32[]{:S(2)}) collective-permute-start(bf16[256,640]{1,0:T(8,128)(2,1)} %param.8), channel_id=1, source_target_pairs={{0,32},{8,40},{16,48},{24,56},{32,64},{40,72},{48,80},{56,88},{64,... | collective-permute-start | bytes 983048 | tf_op jit(solution)/shard_map/ppermute | solution.py:16
  24.3 12.8 %copy-start.17 = (bf16[256,640]{1,0:T(8,128)(2,1)S(1)}, bf16[256,640]{1,0:T(8,128)(2,1)}, u32[]{:S(2)}) copy-start(bf16[256,640]{1,0:T(8,128)(2,1)} %param.8) | copy-start | bytes 983044
  37.1 33.4 %collective-permute-start.5 = (bf16[256,640]{1,0:T(8,128)(2,1)S(1)}, bf16[256,640]{1,0:T(8,128)(2,1)S(1)}, u32[]{:S(2)}, u32[]{:S(2)}) collective-permute-start(bf16[256,640]{1,0:T(8,128)(2,1)S(1)} %copy-done.17), channel_id=1, source_target_pairs={{32,0},{40,8},{48,16},{56,24},{64,32},{72,40},{80,48},{88,56},{96,... | collective-permute-start | bytes 983048 | tf_op jit(solution)/shard_map/ppermute | solution.py:16
  43.0 44.3 %collective-permute-start.6 = (bf16[256,640]{1,0:T(8,128)(2,1)S(1)}, bf16[256,640]{1,0:T(8,128)(2,1)S(1)}, u32[]{:S(2)}, u32[]{:S(2)}) collective-permute-start(bf16[256,640]{1,0:T(8,128)(2,1)S(1)} %copy-done.17), channel_id=1, source_target_pairs={{0,64},{8,72},{16,80},{24,88},{32,96},{40,104},{48,112},{56,120},{... | collective-permute-start | bytes 983048 | tf_op jit(solution)/shard_map/ppermute | solution.py:16
  58.1 31.9 %collective-permute-start.7 = (bf16[256,640]{1,0:T(8,128)(2,1)S(1)}, bf16[256,640]{1,0:T(8,128)(2,1)S(1)}, u32[]{:S(2)}, u32[]{:S(2)}) collective-permute-start(bf16[256,640]{1,0:T(8,128)(2,1)S(1)} %copy-done.17), channel_id=1, source_target_pairs={{64,0},{72,8},{80,16},{88,24},{96,32},{104,40},{112,48},{120,56},{... | collective-permute-start | bytes 983048 | tf_op jit(solution)/shard_map/ppermute | solution.py:16
  61.7 36.6 %collective-permute-start.8 = (bf16[256,640]{1,0:T(8,128)(2,1)S(1)}, bf16[256,640]{1,0:T(8,128)(2,1)S(1)}, u32[]{:S(2)}, u32[]{:S(2)}) collective-permute-start(bf16[256,640]{1,0:T(8,128)(2,1)S(1)} %copy-done.17), channel_id=1, source_target_pairs={{0,128},{8,136},{16,144},{24,152},{32,160},{40,168},{48,176},{56,1... | collective-permute-start | bytes 983048 | tf_op jit(solution)/shard_map/ppermute | solution.py:16
  67.5 33.5 %collective-permute-start.9 = (bf16[256,640]{1,0:T(8,128)(2,1)S(1)}, bf16[256,640]{1,0:T(8,128)(2,1)S(1)}, u32[]{:S(2)}, u32[]{:S(2)}) collective-permute-start(bf16[256,640]{1,0:T(8,128)(2,1)S(1)} %copy-done.17), channel_id=1, source_target_pairs={{128,0},{136,8},{144,16},{152,24},{160,32},{168,40},{176,48},{184,... | collective-permute-start | bytes 983048 | tf_op jit(solution)/shard_map/ppermute | solution.py:16
  70.6 57.8 %collective-permute-start.10 = (bf16[256,640]{1,0:T(8,128)(2,1)S(1)}, bf16[256,640]{1,0:T(8,128)(2,1)S(1)}, u32[]{:S(2)}, u32[]{:S(2)}) collective-permute-start(bf16[256,640]{1,0:T(8,128)(2,1)S(1)} %copy-done.18), channel_id=1, source_target_pairs={{0,8},{8,16},{16,24},{24,32},{32,40},{40,48},{48,56},{56,64},{64,7... | collective-permute-start | bytes 983048 | tf_op jit(solution)/shard_map/ppermute | solution.py:16
  87.3 43.8 %collective-permute-start.11 = (bf16[256,640]{1,0:T(8,128)(2,1)S(1)}, bf16[256,640]{1,0:T(8,128)(2,1)S(1)}, u32[]{:S(2)}, u32[]{:S(2)}) collective-permute-start(bf16[256,640]{1,0:T(8,128)(2,1)S(1)} %copy-done.18), channel_id=1, source_target_pairs={{8,0},{16,8},{24,16},{32,24},{40,32},{48,40},{56,48},{64,56},{72,6... | collective-permute-start | bytes 983048 | tf_op jit(solution)/shard_map/ppermute | solution.py:16
  90.0 46.1 %collective-permute-start.12 = (bf16[256,640]{1,0:T(8,128)(2,1)S(1)}, bf16[256,640]{1,0:T(8,128)(2,1)S(1)}, u32[]{:S(2)}, u32[]{:S(2)}) collective-permute-start(bf16[256,640]{1,0:T(8,128)(2,1)S(1)} %copy-done.18), channel_id=1, source_target_pairs={{0,16},{8,24},{16,32},{24,40},{32,48},{40,56},{48,64},{56,72},{64,... | collective-permute-start | bytes 983048 | tf_op jit(solution)/shard_map/ppermute | solution.py:16
  98.4 41.5 %collective-permute-start.13 = (bf16[256,640]{1,0:T(8,128)(2,1)S(1)}, bf16[256,640]{1,0:T(8,128)(2,1)S(1)}, u32[]{:S(2)}, u32[]{:S(2)}) collective-permute-start(bf16[256,640]{1,0:T(8,128)(2,1)S(1)} %copy-done.18), channel_id=1, source_target_pairs={{16,0},{24,8},{32,16},{40,24},{48,32},{56,40},{64,48},{72,56},{80,... | collective-permute-start | bytes 983048 | tf_op jit(solution)/shard_map/ppermute | solution.py:16
  101.0 46.2 %collective-permute-start.14 = (bf16[256,640]{1,0:T(8,128)(2,1)S(1)}, bf16[256,640]{1,0:T(8,128)(2,1)S(1)}, u32[]{:S(2)}, u32[]{:S(2)}) collective-permute-start(bf16[256,640]{1,0:T(8,128)(2,1)S(1)} %copy-done.18), channel_id=1, source_target_pairs={{0,32},{8,40},{16,48},{24,56},{32,64},{40,72},{48,80},{56,88},{64,... | collective-permute-start | bytes 983048 | tf_op jit(solution)/shard_map/ppermute | solution.py:16
  128.3 23.9 %collective-permute-start.15 = (bf16[256,640]{1,0:T(8,128)(2,1)S(1)}, bf16[256,640]{1,0:T(8,128)(2,1)S(1)}, u32[]{:S(2)}, u32[]{:S(2)}) collective-permute-start(bf16[256,640]{1,0:T(8,128)(2,1)S(1)} %copy-done.18), channel_id=1, source_target_pairs={{32,0},{40,8},{48,16},{56,24},{64,32},{72,40},{80,48},{88,56},{96,... | collective-permute-start | bytes 983048 | tf_op jit(solution)/shard_map/ppermute | solution.py:16
  131.0 25.8 %collective-permute-start.16 = (bf16[256,640]{1,0:T(8,128)(2,1)S(1)}, bf16[256,640]{1,0:T(8,128)(2,1)S(1)}, u32[]{:S(2)}, u32[]{:S(2)}) collective-permute-start(bf16[256,640]{1,0:T(8,128)(2,1)S(1)} %copy-done.18), channel_id=1, source_target_pairs={{0,64},{8,72},{16,80},{24,88},{32,96},{40,104},{48,112},{56,120},{... | collective-permute-start | bytes 983048 | tf_op jit(solution)/shard_map/ppermute | solution.py:16
  136.0 21.5 %collective-permute-start.17 = (bf16[256,640]{1,0:T(8,128)(2,1)S(1)}, bf16[256,640]{1,0:T(8,128)(2,1)S(1)}, u32[]{:S(2)}, u32[]{:S(2)}) collective-permute-start(bf16[256,640]{1,0:T(8,128)(2,1)S(1)} %copy-done.18), channel_id=1, source_target_pairs={{64,0},{72,8},{80,16},{88,24},{96,32},{104,40},{112,48},{120,56},{... | collective-permute-start | bytes 983048 | tf_op jit(solution)/shard_map/ppermute | solution.py:16
  139.9 28.3 %collective-permute-start.18 = (bf16[256,640]{1,0:T(8,128)(2,1)S(1)}, bf16[256,640]{1,0:T(8,128)(2,1)}, u32[]{:S(2)}, u32[]{:S(2)}) collective-permute-start(bf16[256,640]{1,0:T(8,128)(2,1)S(1)} %copy-done.18), channel_id=1, source_target_pairs={{0,128},{8,136},{16,144},{24,152},{32,160},{40,168},{48,176},{56,1... | collective-permute-start | bytes 983048 | tf_op jit(solution)/shard_map/ppermute | solution.py:16
  147.2 22.8 %collective-permute-start.19 = (bf16[256,640]{1,0:T(8,128)(2,1)S(1)}, bf16[256,640]{1,0:T(8,128)(2,1)}, u32[]{:S(2)}, u32[]{:S(2)}) collective-permute-start(bf16[256,640]{1,0:T(8,128)(2,1)S(1)} %copy-done.18), channel_id=1, source_target_pairs={{128,0},{136,8},{144,16},{152,24},{160,32},{168,40},{176,48},{184,... | collective-permute-start | bytes 983048 | tf_op jit(solution)/shard_map/ppermute | solution.py:16
  182.3 1.9 copy-start.2
  182.3 2.0 copy-start.4
  183.8 2.7 copy-start.21
  197.5 4.9 %copy-start.3 = (bf16[2,768,5,128]{3,2,1,0:T(8,128)(2,1)S(1)}, bf16[2,768,5,128]{3,2,1,0:T(8,128)(2,1)}, u32[]{:S(2)}) copy-start(bf16[2,768,5,128]{3,2,1,0:T(8,128)(2,1)} %reshape.151) | copy-start | bytes 5898244
  197.5 4.9 %copy-start.22 = (f32[2,5,128,768]{2,3,1,0:T(8,128)S(1)}, f32[2,5,128,768]{2,3,1,0:T(8,128)}, u32[]{:S(2)}) copy-start(f32[2,5,128,768]{2,3,1,0:T(8,128)} %copy-done.21) | copy-start | bytes 11796484
  203.3 1.3 copy-start
  228.5 52.2 %collective-permute-start.29 = (bf16[2,81920]{1,0:T(2,128)(2,1)}, bf16[2,81920]{1,0:T(2,128)(2,1)S(1)}, u32[]{:S(2)}, u32[]{:S(2)}) collective-permute-start(bf16[2,81920]{1,0:T(2,128)(2,1)} %get-tuple-element.32), channel_id=1, source_target_pairs={{0,128},{8,136},{16,144},{24,152},{32,160},{40,168},{48,176},{56,1... | collective-permute-start | bytes 983048 | tf_op jit(solution)/shard_map/ppermute | solution.py:16
  229.8 52.9 %collective-permute-start.28 = (bf16[2,81920]{1,0:T(2,128)(2,1)}, bf16[2,81920]{1,0:T(2,128)(2,1)S(1)}, u32[]{:S(2)}, u32[]{:S(2)}) collective-permute-start(bf16[2,81920]{1,0:T(2,128)(2,1)} %get-tuple-element.33), channel_id=1, source_target_pairs={{128,0},{136,8},{144,16},{152,24},{160,32},{168,40},{176,48},{184,... | collective-permute-start | bytes 983048 | tf_op jit(solution)/shard_map/ppermute | solution.py:16
  231.1 64.6 %collective-permute-start.27 = (bf16[2,81920]{1,0:T(2,128)(2,1)}, bf16[2,81920]{1,0:T(2,128)(2,1)S(1)}, u32[]{:S(2)}, u32[]{:S(2)}) collective-permute-start(bf16[2,81920]{1,0:T(2,128)(2,1)} %get-tuple-element.34), channel_id=1, source_target_pairs={{0,64},{8,72},{16,80},{24,88},{32,96},{40,104},{48,112},{56,120},{... | collective-permute-start | bytes 983048 | tf_op jit(solution)/shard_map/ppermute | solution.py:16
  246.7 50.9 %collective-permute-start.26 = (bf16[2,81920]{1,0:T(2,128)(2,1)}, bf16[2,81920]{1,0:T(2,128)(2,1)S(1)}, u32[]{:S(2)}, u32[]{:S(2)}) collective-permute-start(bf16[2,81920]{1,0:T(2,128)(2,1)} %get-tuple-element.35), channel_id=1, source_target_pairs={{64,0},{72,8},{80,16},{88,24},{96,32},{104,40},{112,48},{120,56},{... | collective-permute-start | bytes 983048 | tf_op jit(solution)/shard_map/ppermute | solution.py:16
  248.7 62.3 %collective-permute-start.25 = (bf16[2,81920]{1,0:T(2,128)(2,1)}, bf16[2,81920]{1,0:T(2,128)(2,1)}, u32[]{:S(2)}, u32[]{:S(2)}) collective-permute-start(bf16[2,81920]{1,0:T(2,128)(2,1)} %get-tuple-element.36), channel_id=1, source_target_pairs={{0,32},{8,40},{16,48},{24,56},{32,64},{40,72},{48,80},{56,88},{64,... | collective-permute-start | bytes 983048 | tf_op jit(solution)/shard_map/ppermute | solution.py:16
  271.5 9.1 %copy-start.15 = (bf16[2,81920]{1,0:T(2,128)(2,1)S(1)}, bf16[2,81920]{1,0:T(2,128)(2,1)}, u32[]{:S(2)}) copy-start(bf16[2,81920]{1,0:T(2,128)(2,1)} %get-tuple-element.37) | copy-start | bytes 983044
  271.5 11.2 %copy-start.14 = (bf16[2,81920]{1,0:T(2,128)(2,1)S(1)}, bf16[2,81920]{1,0:T(2,128)(2,1)}, u32[]{:S(2)}) copy-start(bf16[2,81920]{1,0:T(2,128)(2,1)} %get-tuple-element.38) | copy-start | bytes 983044
  271.5 24.2 %copy-start.13 = (bf16[2,81920]{1,0:T(2,128)(2,1)S(1)}, bf16[2,81920]{1,0:T(2,128)(2,1)}, u32[]{:S(2)}) copy-start(bf16[2,81920]{1,0:T(2,128)(2,1)} %get-tuple-element.39) | copy-start | bytes 983044
  271.5 26.2 %copy-start.12 = (bf16[2,81920]{1,0:T(2,128)(2,1)S(1)}, bf16[2,81920]{1,0:T(2,128)(2,1)}, u32[]{:S(2)}) copy-start(bf16[2,81920]{1,0:T(2,128)(2,1)} %get-tuple-element.40) | copy-start | bytes 983044
  271.5 39.5 %copy-start.10 = (bf16[2,81920]{1,0:T(2,128)(2,1)S(1)}, bf16[2,81920]{1,0:T(2,128)(2,1)}, u32[]{:S(2)}) copy-start(bf16[2,81920]{1,0:T(2,128)(2,1)} %get-tuple-element.31) | copy-start | bytes 983044
  280.6 59.5 %copy-start.1 = (bf16[2,5,128,768]{2,3,1,0:T(8,128)(2,1)S(1)}, bf16[2,5,128,768]{2,3,1,0:T(8,128)(2,1)}, u32[]{:S(2)}) copy-start(bf16[2,5,128,768]{2,3,1,0:T(8,128)(2,1)} %copy-done) | copy-start | bytes 5898244
  280.6 36.2 %collective-permute-start.24 = (bf16[2,81920]{1,0:T(2,128)(2,1)S(1)}, bf16[2,81920]{1,0:T(2,128)(2,1)S(1)}, u32[]{:S(2)}, u32[]{:S(2)}) collective-permute-start(bf16[2,81920]{1,0:T(2,128)(2,1)S(1)} %copy-done.15), channel_id=1, source_target_pairs={{32,0},{40,8},{48,16},{56,24},{64,32},{72,40},{80,48},{88,56},{96,... | collective-permute-start | bytes 983048 | tf_op jit(solution)/shard_map/ppermute | solution.py:16
  282.7 36.1 %collective-permute-start.23 = (bf16[2,81920]{1,0:T(2,128)(2,1)S(1)}, bf16[2,81920]{1,0:T(2,128)(2,1)S(1)}, u32[]{:S(2)}, u32[]{:S(2)}) collective-permute-start(bf16[2,81920]{1,0:T(2,128)(2,1)S(1)} %copy-done.14), channel_id=1, source_target_pairs={{0,16},{8,24},{16,32},{24,40},{32,48},{40,56},{48,64},{56,72},{64,... | collective-permute-start | bytes 983048 | tf_op jit(solution)/shard_map/ppermute | solution.py:16
  295.7 25.6 %collective-permute-start.22 = (bf16[2,81920]{1,0:T(2,128)(2,1)S(1)}, bf16[2,81920]{1,0:T(2,128)(2,1)S(1)}, u32[]{:S(2)}, u32[]{:S(2)}) collective-permute-start(bf16[2,81920]{1,0:T(2,128)(2,1)S(1)} %copy-done.13), channel_id=1, source_target_pairs={{16,0},{24,8},{32,16},{40,24},{48,32},{56,40},{64,48},{72,56},{80,... | collective-permute-start | bytes 983048 | tf_op jit(solution)/shard_map/ppermute | solution.py:16
  297.6 40.5 %copy-start.5 = (bf16[2,81920]{1,0:T(2,128)(2,1)}, bf16[2,81920]{1,0:T(2,128)(2,1)S(1)}, u32[]{:S(2)}) copy-start(bf16[2,81920]{1,0:T(2,128)(2,1)S(1)} %collective-permute-done.26) | copy-start | bytes 983044
  297.7 38.1 %collective-permute-start.21 = (bf16[2,81920]{1,0:T(2,128)(2,1)S(1)}, bf16[2,81920]{1,0:T(2,128)(2,1)S(1)}, u32[]{:S(2)}, u32[]{:S(2)}) collective-permute-start(bf16[2,81920]{1,0:T(2,128)(2,1)S(1)} %copy-done.12), channel_id=1, source_target_pairs={{0,8},{8,16},{16,24},{24,32},{32,40},{40,48},{48,56},{56,64},{64,7... | collective-permute-start | bytes 983048 | tf_op jit(solution)/shard_map/ppermute | solution.py:16
  311.0 27.1 %collective-permute-start.20 = (bf16[2,81920]{1,0:T(2,128)(2,1)S(1)}, bf16[2,81920]{1,0:T(2,128)(2,1)S(1)}, u32[]{:S(2)}, u32[]{:S(2)}) collective-permute-start(bf16[2,81920]{1,0:T(2,128)(2,1)S(1)} %copy-done.10), channel_id=1, source_target_pairs={{8,0},{16,8},{24,16},{32,24},{40,32},{48,40},{56,48},{64,56},{72,6... | collective-permute-start | bytes 983048 | tf_op jit(solution)/shard_map/ppermute | solution.py:16
  316.8 23.3 %copy-start.6 = (bf16[2,81920]{1,0:T(2,128)(2,1)}, bf16[2,81920]{1,0:T(2,128)(2,1)S(1)}, u32[]{:S(2)}) copy-start(bf16[2,81920]{1,0:T(2,128)(2,1)S(1)} %collective-permute-done.24) | copy-start | bytes 983044
  316.8 37.5 %collective-permute-start.39 = (bf16[2,81920]{1,0:T(2,128)(2,1)}, bf16[2,81920]{1,0:T(2,128)(2,1)}, u32[]{:S(2)}, u32[]{:S(2)}) collective-permute-start(bf16[2,81920]{1,0:T(2,128)(2,1)} %get-tuple-element.22), channel_id=1, source_target_pairs={{0,128},{8,136},{16,144},{24,152},{32,160},{40,168},{48,176},{56,1... | collective-permute-start | bytes 983048 | tf_op jit(solution)/shard_map/ppermute | solution.py:16
  318.8 21.3 %copy-start.7 = (bf16[2,81920]{1,0:T(2,128)(2,1)}, bf16[2,81920]{1,0:T(2,128)(2,1)S(1)}, u32[]{:S(2)}) copy-start(bf16[2,81920]{1,0:T(2,128)(2,1)S(1)} %collective-permute-done.23) | copy-start | bytes 983044
  318.8 37.3 %collective-permute-start.38 = (bf16[2,81920]{1,0:T(2,128)(2,1)}, bf16[2,81920]{1,0:T(2,128)(2,1)}, u32[]{:S(2)}, u32[]{:S(2)}) collective-permute-start(bf16[2,81920]{1,0:T(2,128)(2,1)} %get-tuple-element.23), channel_id=1, source_target_pairs={{128,0},{136,8},{144,16},{152,24},{160,32},{168,40},{176,48},{184,... | collective-permute-start | bytes 983048 | tf_op jit(solution)/shard_map/ppermute | solution.py:16
  321.3 18.8 %copy-start.8 = (bf16[2,81920]{1,0:T(2,128)(2,1)}, bf16[2,81920]{1,0:T(2,128)(2,1)S(1)}, u32[]{:S(2)}) copy-start(bf16[2,81920]{1,0:T(2,128)(2,1)S(1)} %collective-permute-done.22) | copy-start | bytes 983044
  321.3 47.0 %collective-permute-start.37 = (bf16[2,81920]{1,0:T(2,128)(2,1)}, bf16[2,81920]{1,0:T(2,128)(2,1)}, u32[]{:S(2)}, u32[]{:S(2)}) collective-permute-start(bf16[2,81920]{1,0:T(2,128)(2,1)} %get-tuple-element.24), channel_id=1, source_target_pairs={{0,64},{8,72},{16,80},{24,88},{32,96},{40,104},{48,112},{56,120},{... | collective-permute-start | bytes 983048 | tf_op jit(solution)/shard_map/ppermute | solution.py:16
  335.7 4.4 %copy-start.9 = (bf16[2,81920]{1,0:T(2,128)(2,1)}, bf16[2,81920]{1,0:T(2,128)(2,1)S(1)}, u32[]{:S(2)}) copy-start(bf16[2,81920]{1,0:T(2,128)(2,1)S(1)} %collective-permute-done.21) | copy-start | bytes 983044
  335.7 34.5 %collective-permute-start.36 = (bf16[2,81920]{1,0:T(2,128)(2,1)}, bf16[2,81920]{1,0:T(2,128)(2,1)}, u32[]{:S(2)}, u32[]{:S(2)}) collective-permute-start(bf16[2,81920]{1,0:T(2,128)(2,1)} %get-tuple-element.25), channel_id=1, source_target_pairs={{64,0},{72,8},{80,16},{88,24},{96,32},{104,40},{112,48},{120,56},{... | collective-permute-start | bytes 983048 | tf_op jit(solution)/shard_map/ppermute | solution.py:16
  338.2 2.0 copy-start.11
  338.2 42.1 %collective-permute-start.35 = (bf16[2,81920]{1,0:T(2,128)(2,1)}, bf16[2,81920]{1,0:T(2,128)(2,1)}, u32[]{:S(2)}, u32[]{:S(2)}) collective-permute-start(bf16[2,81920]{1,0:T(2,128)(2,1)} %get-tuple-element.26), channel_id=1, source_target_pairs={{0,32},{8,40},{16,48},{24,56},{32,64},{40,72},{48,80},{56,88},{64,... | collective-permute-start | bytes 983048 | tf_op jit(solution)/shard_map/ppermute | solution.py:16
  354.2 33.3 %collective-permute-start.34 = (bf16[2,81920]{1,0:T(2,128)(2,1)}, bf16[2,81920]{1,0:T(2,128)(2,1)S(1)}, u32[]{:S(2)}, u32[]{:S(2)}) collective-permute-start(bf16[2,81920]{1,0:T(2,128)(2,1)} %get-tuple-element.27), channel_id=1, source_target_pairs={{32,0},{40,8},{48,16},{56,24},{64,32},{72,40},{80,48},{88,56},{96,... | collective-permute-start | bytes 983048 | tf_op jit(solution)/shard_map/ppermute | solution.py:16
  356.2 33.2 %collective-permute-start.33 = (bf16[2,81920]{1,0:T(2,128)(2,1)}, bf16[2,81920]{1,0:T(2,128)(2,1)S(1)}, u32[]{:S(2)}, u32[]{:S(2)}) collective-permute-start(bf16[2,81920]{1,0:T(2,128)(2,1)} %get-tuple-element.28), channel_id=1, source_target_pairs={{0,16},{8,24},{16,32},{24,40},{32,48},{40,56},{48,64},{56,72},{64,... | collective-permute-start | bytes 983048 | tf_op jit(solution)/shard_map/ppermute | solution.py:16
  368.3 21.1 %collective-permute-start.32 = (bf16[2,81920]{1,0:T(2,128)(2,1)}, bf16[2,81920]{1,0:T(2,128)(2,1)S(1)}, u32[]{:S(2)}, u32[]{:S(2)}) collective-permute-start(bf16[2,81920]{1,0:T(2,128)(2,1)} %get-tuple-element.29), channel_id=1, source_target_pairs={{16,0},{24,8},{32,16},{40,24},{48,32},{56,40},{64,48},{72,56},{80,... | collective-permute-start | bytes 983048 | tf_op jit(solution)/shard_map/ppermute | solution.py:16
  370.2 23.3 %collective-permute-start.31 = (bf16[2,81920]{1,0:T(2,128)(2,1)}, bf16[2,81920]{1,0:T(2,128)(2,1)S(1)}, u32[]{:S(2)}, u32[]{:S(2)}) collective-permute-start(bf16[2,81920]{1,0:T(2,128)(2,1)} %get-tuple-element.30), channel_id=1, source_target_pairs={{0,8},{8,16},{16,24},{24,32},{32,40},{40,48},{48,56},{56,64},{64,7... | collective-permute-start | bytes 983048 | tf_op jit(solution)/shard_map/ppermute | solution.py:16
  380.3 27.8 %collective-permute-start.30 = (bf16[2,81920]{1,0:T(2,128)(2,1)}, bf16[2,81920]{1,0:T(2,128)(2,1)S(1)}, u32[]{:S(2)}, u32[]{:S(2)}) collective-permute-start(bf16[2,81920]{1,0:T(2,128)(2,1)} %get-tuple-element.21), channel_id=1, source_target_pairs={{8,0},{16,8},{24,16},{32,24},{40,32},{48,40},{56,48},{64,56},{72,6... | collective-permute-start | bytes 983048 | tf_op jit(solution)/shard_map/ppermute | solution.py:16
